TPU v7x, 32 devices: a whole 2x2x4 slice. The times are simulated.
32 devices in a mesh: dp: 8 (over z, y), tensor: 4 (over x, core).
Axes of the slice: x: 2, y: 2, z: 4, core: 2. Of those that a mesh axis runs over, the one named last changes fastest.
Arguments:
- tokens: bfloat16 [16384, 768], P(('dp', 'tensor')), may hold values from -6 to 6
- time_emb: bfloat16 [16, 128], P('dp'), may hold values from -5 to 5
- prefix_len: int32 [16], P('dp'), may hold values from 0 to 511
- noise_mask: int32 [16384], P(('dp', 'tensor')), may hold values 0 or 1
- mask_embed: bfloat16 [768], replicated, may hold values from -5 to 5
- gain_attn: bfloat16 [768], replicated, may hold values from 0.25 to 1.75
- gain_mlp: bfloat16 [768], replicated, may hold values from 0.25 to 1.75
- ada_weight: bfloat16 [128, 4608], replicated, may hold values from -0.5 to 0.5
- ada_bias: bfloat16 [4608], replicated, may hold values from -3 to 3
- qkv_weight: bfloat16 [768, 3, 768], P(None, None, 'tensor'), may hold values from -0.21875 to 0.21875
- out_weight: bfloat16 [768, 768], P('tensor'), may hold values from -0.75 to 0.75
- up_weight: bfloat16 [768, 3072], P(None, 'tensor'), may hold values from -0.21875 to 0.21875
- up_bias: bfloat16 [3072], P('tensor'), may hold values from -3 to 3
- down_weight: bfloat16 [3072, 768], P('tensor'), may hold values from -0.109375 to 0.109375
- down_bias: bfloat16 [768], replicated, may hold values from -3 to 3
- cotangent: bfloat16 [16384, 768], P(('dp', 'tensor')), may hold values from -6 to 6
Outputs:
- output: bfloat16 [16384, 768], P(('dp', 'tensor'))
- grad_tokens: float32 [16384, 768], P(('dp', 'tensor'))
- grad_time: float32 [16, 128], P('dp')
- grad_mask_embed: float32 [768], replicated
- grad_gain_attn: float32 [768], replicated
- grad_gain_mlp: float32 [768], replicated
- grad_ada_weight: float32 [128, 4608], replicated
- grad_ada_bias: float32 [4608], replicated
- grad_qkv: float32 [768, 3, 768], P(None, None, 'tensor')
- grad_out: float32 [768, 768], P('tensor')
- grad_up: float32 [768, 3072], P(None, 'tensor')
- grad_up_bias: float32 [3072], P('tensor')
- grad_down: float32 [3072, 768], P('tensor')
- grad_down_bias: float32 [768], replicated
All inputs are finite; a program needn't handle non-finite values. No bound on the sum of `noise_mask` on one device may be relied on, other than what follows from the above.
Results may differ from a plain program's by a relative error of at most 0.012.
The roundings to bfloat16 on the way count: a program that leaves them out, or rounds other values in their place, can miss the bound.
Values may be sent and summed in bfloat16 or wider, within the bound.
A program may use at most 128 MiB of HBM per device.

v0:
```python
import jax
import jax.numpy as jnp
from jax import lax
from jax.sharding import PartitionSpec as P

HD = 64
LEN = 1024


norm_eps = 1e-05
gelu_coef = 0.7978845608028654
cubic_coef = 0.044715
score_scale = 0.125


def matmul_high(left, right):
    return jnp.dot(left, right, precision=lax.Precision.HIGHEST, preferred_element_type=jnp.float32)


def contract_rows(left, right):
    return lax.dot_general(
        left, right, (((0,), (0,)), ((), ())), preferred_element_type=jnp.float32
    )


def contract_precise(left, right):
    return lax.dot_general(
        left,
        right,
        (((0,), (0,)), ((), ())),
        precision=lax.Precision.HIGHEST,
        preferred_element_type=jnp.float32,
    )


def contract_cols(left, right):
    return lax.dot_general(
        left, right, (((1,), (1,)), ((), ())), preferred_element_type=jnp.float32
    )


def normalize(values):
    centered = values - jnp.mean(values, axis=-1, keepdims=True)
    scale_inv = lax.rsqrt(jnp.mean(centered * centered, axis=-1, keepdims=True) + norm_eps)
    return (centered * scale_inv, scale_inv)


def layer_back(grad_norm, normed, scale_inv):
    mean_grad = jnp.mean(grad_norm, axis=-1, keepdims=True)
    mean_cross = jnp.mean(grad_norm * normed, axis=-1, keepdims=True)
    return scale_inv * (grad_norm - mean_grad - normed * mean_cross)


def rotate_half(vectors):
    half_size = vectors.shape[-1] // 2
    return jnp.concatenate([-vectors[..., half_size:], vectors[..., :half_size]], axis=-1)


def rotate_back(vectors):
    half_size = vectors.shape[-1] // 2
    return jnp.concatenate([vectors[..., half_size:], -vectors[..., :half_size]], axis=-1)


def rotary_tables(seq_len, head_size):
    frequency = 10000.0 ** (-2.0 * jnp.arange(head_size // 2, dtype=jnp.float32) / head_size)
    angles = jnp.arange(seq_len, dtype=jnp.float32)[:, None] * frequency[None, :]
    angles = jnp.concatenate([angles, angles], axis=-1)
    return (jnp.cos(angles), jnp.sin(angles))


def gelu_tanh(values):
    return (
        0.5
        * values
        * (1.0 + jnp.tanh(gelu_coef * (values + cubic_coef * values * values * values)))
    )


def gelu_slope(values):
    tangent = jnp.tanh(gelu_coef * (values + cubic_coef * values * values * values))
    return 0.5 * (1.0 + tangent) + 0.5 * values * (1.0 - tangent * tangent) * gelu_coef * (
        1.0 + 3.0 * cubic_coef * values * values
    )


def attend(operands):
    queries, key_rows, value_rows = operands
    scores = (
        jnp.einsum("qhe,khe->hqk", queries, key_rows, preferred_element_type=jnp.float32)
        * score_scale
    )
    row_max = jnp.max(scores, axis=-1, keepdims=True)
    weights = jnp.exp(scores - row_max)
    denominator = jnp.sum(weights, axis=-1, keepdims=True)
    probability = (weights / denominator).astype(jnp.bfloat16)
    attended = jnp.einsum(
        "hqk,khe->qhe", probability, value_rows, preferred_element_type=jnp.float32
    )
    return (attended, (row_max + jnp.log(denominator))[..., 0])


def attend_back(operands):
    queries, key_rows, value_rows, grad_att, log_total = operands
    scores = (
        jnp.einsum("qhe,khe->hqk", queries, key_rows, preferred_element_type=jnp.float32)
        * score_scale
    )
    probability = jnp.exp(scores - log_total[..., None])
    grad_prob = jnp.einsum("qhe,khe->hqk", grad_att, value_rows, preferred_element_type=jnp.float32)
    inner_sum = jnp.sum(probability * grad_prob, axis=-1, keepdims=True)
    grad_scores = (probability * (grad_prob - inner_sum)).astype(jnp.bfloat16)
    grad_query = (
        jnp.einsum("hqk,khe->qhe", grad_scores, key_rows, preferred_element_type=jnp.float32)
        * score_scale
    )
    grad_key = (
        jnp.einsum("hqk,qhe->khe", grad_scores, queries, preferred_element_type=jnp.float32)
        * score_scale
    )
    grad_value = jnp.einsum(
        "hqk,qhe->khe",
        probability.astype(jnp.bfloat16),
        grad_att,
        preferred_element_type=jnp.float32,
    )
    return (grad_query, grad_key, grad_value)


def per_device(
    tokens,
    time_emb,
    prefix_len,
    noise_mask,
    mask_embed,
    gain_attn,
    gain_mlp,
    ada_weight,
    ada_bias,
    qkv_weight,
    out_weight,
    up_weight,
    up_bias,
    down_weight,
    down_bias,
    cotangent,
):
    row_count = tokens.shape[0]
    seq_count = time_emb.shape[0]
    local_width = qkv_weight.shape[2]
    head_count = local_width // HD
    group_rows = row_count * lax.axis_size("tensor")
    row_place = lax.axis_index("tensor") * row_count + jnp.arange(row_count, dtype=jnp.int32)
    position = row_place % LEN
    sequence = row_place // LEN
    belongs = sequence[:, None] == jnp.arange(seq_count, dtype=jnp.int32)[None, :]
    member = belongs.astype(jnp.float32)
    prefix_row = jnp.sum(jnp.where(belongs, prefix_len[None, :], 0), axis=1)
    noised = (noise_mask == 1) & (position >= prefix_row)
    inputs = jnp.where(
        noised[:, None], mask_embed.astype(jnp.float32)[None, :], tokens.astype(jnp.float32)
    )
    time_value = time_emb.astype(jnp.float32)
    silu_time = jax.nn.silu(time_value)
    ada_full = ada_weight.astype(jnp.float32)
    modulation = matmul_high(silu_time, ada_full) + ada_bias.astype(jnp.float32)
    per_row = matmul_high(member, modulation)
    shift_attn, scale_attn, gate_attn, shift_mlp, scale_mlp, gate_mlp = jnp.split(
        per_row, 6, axis=1
    )
    gain_one = gain_attn.astype(jnp.float32)
    gain_two = gain_mlp.astype(jnp.float32)
    norm_one, inv_one = normalize(inputs)
    pre_one = norm_one * gain_one
    hidden_one = (pre_one * (1.0 + scale_attn) + shift_attn).astype(jnp.bfloat16)
    full_one = lax.all_gather(hidden_one, "tensor", axis=0, tiled=True)
    projected = jnp.einsum("rd,dcf->rcf", full_one, qkv_weight, preferred_element_type=jnp.float32)
    projected = projected.reshape(seq_count, LEN, 3, head_count, HD)
    cosine, sine = rotary_tables(LEN, HD)
    cosine = cosine[None, :, None, :]
    sine = sine[None, :, None, :]
    raw_query = projected[:, :, 0]
    raw_key = projected[:, :, 1]
    queries = (raw_query * cosine + rotate_half(raw_query) * sine).astype(jnp.bfloat16)
    key_rows = (raw_key * cosine + rotate_half(raw_key) * sine).astype(jnp.bfloat16)
    value_rows = projected[:, :, 2].astype(jnp.bfloat16)
    attended, log_total = lax.map(attend, (queries, key_rows, value_rows))
    attended_low = attended.reshape(group_rows, local_width).astype(jnp.bfloat16)
    partial_attn = jnp.dot(attended_low, out_weight, preferred_element_type=jnp.float32)
    branch_attn = lax.psum_scatter(partial_attn, "tensor", scatter_dimension=0, tiled=True)
    mixed = inputs + gate_attn * branch_attn
    norm_two, inv_two = normalize(mixed)
    pre_two = norm_two * gain_two
    hidden_two = (pre_two * (1.0 + scale_mlp) + shift_mlp).astype(jnp.bfloat16)
    bias_down = down_bias.astype(jnp.float32)
    grad_final = cotangent.astype(jnp.float32)
    full_two = lax.all_gather(hidden_two, "tensor", axis=0, tiled=True)
    upper = jnp.dot(full_two, up_weight, preferred_element_type=jnp.float32) + up_bias.astype(
        jnp.float32
    )
    active = gelu_tanh(upper).astype(jnp.bfloat16)
    partial_mlp = jnp.dot(active, down_weight, preferred_element_type=jnp.float32)
    branch_mlp = (
        lax.psum_scatter(
            partial_mlp.astype(jnp.bfloat16), "tensor", scatter_dimension=0, tiled=True
        ).astype(jnp.float32)
        + bias_down
    )
    grad_branch_mlp = (gate_mlp * grad_final).astype(jnp.bfloat16)
    full_grad_two = lax.all_gather(grad_branch_mlp, "tensor", axis=0, tiled=True)
    grad_down = contract_rows(active, full_grad_two)
    grad_active = contract_cols(full_grad_two, down_weight)
    grad_upper = (grad_active * gelu_slope(upper)).astype(jnp.bfloat16)
    grad_up = contract_rows(full_two, grad_upper)
    grad_up_bias = jnp.sum(grad_upper.astype(jnp.float32), axis=0)
    grad_hidden_two = lax.psum_scatter(
        contract_cols(grad_upper, up_weight), "tensor", scatter_dimension=0, tiled=True
    )
    output = (mixed + gate_mlp * branch_mlp).astype(jnp.bfloat16)
    grad_down_bias = jnp.sum(grad_branch_mlp.astype(jnp.float32), axis=0)
    grad_norm_two = grad_hidden_two * (1.0 + scale_mlp) * gain_two
    grad_mixed = grad_final + layer_back(grad_norm_two, norm_two, inv_two)
    grad_gain_two = jnp.sum(grad_hidden_two * (1.0 + scale_mlp) * norm_two, axis=0)
    grad_branch_attn = (gate_attn * grad_mixed).astype(jnp.bfloat16)
    full_grad_one = lax.all_gather(grad_branch_attn, "tensor", axis=0, tiled=True)
    grad_out_weight = contract_rows(attended_low, full_grad_one)
    grad_attended = (
        contract_cols(full_grad_one, out_weight)
        .astype(jnp.bfloat16)
        .reshape(seq_count, LEN, head_count, HD)
    )
    grad_query, grad_key, grad_value = lax.map(
        attend_back, (queries, key_rows, value_rows, grad_attended, log_total)
    )
    grad_query = grad_query * cosine + rotate_back(grad_query * sine)
    grad_key = grad_key * cosine + rotate_back(grad_key * sine)
    grad_projected = (
        jnp.stack([grad_query, grad_key, grad_value], axis=2)
        .reshape(group_rows, 3, local_width)
        .astype(jnp.bfloat16)
    )
    grad_qkv = jnp.einsum(
        "rd,rcf->dcf", full_one, grad_projected, preferred_element_type=jnp.float32
    )
    partial_back = jnp.einsum(
        "rcf,dcf->rd", grad_projected, qkv_weight, preferred_element_type=jnp.float32
    )
    grad_hidden_one = lax.psum_scatter(partial_back, "tensor", scatter_dimension=0, tiled=True)
    grad_norm_one = grad_hidden_one * (1.0 + scale_attn) * gain_one
    grad_inputs = grad_mixed + layer_back(grad_norm_one, norm_one, inv_one)
    grad_gain_one = jnp.sum(grad_hidden_one * (1.0 + scale_attn) * norm_one, axis=0)
    grad_tokens = jnp.where(noised[:, None], 0.0, grad_inputs)
    grad_mask = jnp.sum(jnp.where(noised[:, None], grad_inputs, 0.0), axis=0)
    row_terms = jnp.concatenate(
        [
            grad_hidden_one,
            grad_hidden_one * pre_one,
            grad_mixed * branch_attn,
            grad_hidden_two,
            grad_hidden_two * pre_two,
            grad_final * branch_mlp,
        ],
        axis=1,
    )
    grad_modulation = contract_precise(member, row_terms)
    sigmoid_time = jax.nn.sigmoid(time_value)
    time_term = (
        matmul_high(grad_modulation, ada_full.T)
        * sigmoid_time
        * (1.0 + time_value * (1.0 - sigmoid_time))
    )
    grad_time = lax.psum(time_term, "tensor")
    grad_ada_weight = contract_precise(silu_time, grad_modulation)
    grad_ada_bias = jnp.sum(grad_modulation, axis=0)
    small_sums = lax.psum(
        (grad_ada_weight, grad_ada_bias, grad_gain_one, grad_gain_two, grad_down_bias, grad_mask),
        ("dp", "tensor"),
    )
    large_sums = lax.psum((grad_qkv, grad_out_weight, grad_up, grad_up_bias, grad_down), "dp")
    return (
        output,
        grad_tokens,
        grad_time,
        small_sums[5],
        small_sums[2],
        small_sums[3],
        small_sums[0],
        small_sums[1],
        large_sums[0],
        large_sums[1],
        large_sums[2],
        large_sums[3],
        large_sums[4],
        small_sums[4],
    )


def solution(mesh):
    in_specs = (
        P(("dp", "tensor"), None),
        P("dp", None),
        P("dp"),
        P(("dp", "tensor")),
        P(),
        P(),
        P(),
        P(),
        P(),
        P(None, None, "tensor"),
        P("tensor", None),
        P(None, "tensor"),
        P("tensor"),
        P("tensor", None),
        P(),
        P(("dp", "tensor"), None),
    )
    out_specs = (
        P(("dp", "tensor"), None),
        P(("dp", "tensor"), None),
        P("dp", None),
        P(),
        P(),
        P(),
        P(),
        P(),
        P(None, None, "tensor"),
        P("tensor", None),
        P(None, "tensor"),
        P("tensor"),
        P("tensor", None),
        P(),
    )
    return jax.shard_map(
        per_device, mesh=mesh, in_specs=in_specs, out_specs=out_specs, check_vma=False
    )
```

profile of v0, /device:TPU:0, one launch (start us, length us, event | category | flops | bytes accessed | tf_op | source)
XLA Modules:
  0.0 898.7 jit_solution(3273983621697902212)
XLA Ops:
  13.4 3.9 fusion.77
  17.3 3.7 copy-done.3
  28.1 26.2 %all-gather.5.cloned.1.call-done = bf16[2048,768]{1,0:T(8,128)(2,1)} async-done(((bf16[512,768]{1,0:T(8,128)(2,1)}), bf16[2048,768]{1,0:T(8,128)(2,1)}) %all-gather.5.cloned.1.call-update) | async-done | bytes 3145744 | tf_op jit(solution)/shard_map/all_gather | solution.py:175
  54.4 6.1 fusion.101
  60.5 7.4 reshape.184
  69.9 3.0 fusion.96
  77.3 16.6 %while.28 = (s32[]{:T(128)}, bf16[2,1024,3,64]{1,3,2,0:T(8,128)(2,1)}, f32[2,3,1024]{2,1,0:T(4,128)}, bf16[2,1024,3,64]{1,3,2,0:T(8,128)(2,1)}, bf16[2,1024,3,64...) while((s32[]{:T(128)}, bf16[2,1024,3,64]{1,3,2,0:T(8,128)(2,1)}, ...), condition=%wide.region_6.7_spmd.clone, body=%wide.region_3.6_spmd.sunk.clone | while | flops 833614848 | bytes 49469660 | solution.py:186
  81.6 2.7 fusion.172
  97.0 3.6 fusion.102
  101.3 57.9 %reduce-scatter.5.cloned.1.call-done = f32[512,768]{1,0:T(8,128)} async-done(((f32[2048,768]{1,0:T(8,128)}), f32[512,768]{1,0:T(8,128)}) %reduce-scatter.5.cloned.1.call-update) | async-done | bytes 1572880 | tf_op jit(solution)/shard_map/reduce_scatter | solution.py:189
  163.2 4.5 convert_reduce_fusion.1
  169.6 26.9 %all-gather.7.cloned.1.call-done = bf16[2048,768]{1,0:T(8,128)(2,1)} async-done(((bf16[512,768]{1,0:T(8,128)(2,1)}), bf16[2048,768]{1,0:T(8,128)(2,1)}) %all-gather.7.cloned.1.call-update) | async-done | bytes 3145744 | tf_op jit(solution)/shard_map/all_gather | solution.py:196
  196.5 9.4 %multiply_convert_fusion.1 = (bf16[2048,768]{1,0:T(8,128)(2,1)}, f32[2048,768]{1,0:T(8,128)}) fusion(f32[768]{0:T(1024)S(1)} %convert_element_type.104, bf16[2048,768]{1,0:T(8,128)(2,1)} %all-gather.7.cloned.1.call-done, bf16[768,768]{1,0:T(8,128)(2,1)S(1)} %copy-done), kind=kOutput, calls=%fused_computation.64 | convolution fusion | flops 2431647744 | bytes 13765632 | tf_op jit(solution)/shard_map/dot_general | solution.py:197
  205.9 21.3 %all-gather.9.cloned.1.call-done = bf16[2048,768]{1,0:T(8,128)(2,1)} async-done(((bf16[512,768]{1,0:T(8,128)(2,1)}), bf16[2048,768]{1,0:T(8,128)(2,1)}) %all-gather.9.cloned.1.call-update) | async-done | bytes 3145744 | tf_op jit(solution)/shard_map/all_gather | solution.py:209
  227.1 9.5 %convert_reduce_fusion = (f32[768]{0:T(1024)}, bf16[2048,768]{1,0:T(8,128)(2,1)S(1)}) fusion(f32[2048,768]{1,0:T(8,128)} %get-tuple-element.211, f32[768]{0:T(1024)S(1)} %convert_element_type.104, bf16[2048,768]{1,0:T(8,128)(2,1)} %all-gather.9.cloned.1.call-done, bf16[768,768]{1,0:T(8,128)(2,1)} %param.33), kind=kOutput, calls=%fused_computation.63 | convolution fusion | flops 2450521344 | bytes 13768704 | tf_op jit(solution)/shard_map/dot_general | solution.py:37
  238.3 4.5 fusion.103
  244.1 6.1 convolution_convert_fusion
  250.9 50.4 %reduce-scatter.9.cloned.1.call-done = f32[512,768]{1,0:T(8,128)} async-done(((f32[2048,768]{1,0:T(8,128)}), f32[512,768]{1,0:T(8,128)}) %reduce-scatter.9.cloned.1.call-update) | async-done | bytes 1572880 | tf_op jit(solution)/shard_map/reduce_scatter | solution.py:215
  301.3 4.7 multiply_reduce_fusion.2
  306.0 35.7 %reduce-scatter.7.cloned.1.call-done = bf16[512,768]{1,0:T(8,128)(2,1)} async-done(((bf16[2048,768]{1,0:T(8,128)(2,1)}), bf16[512,768]{1,0:T(8,128)(2,1)}) %reduce-scatter.7.cloned.1.call-update) | async-done | bytes 786448 | tf_op jit(solution)/shard_map/reduce_scatter | solution.py:203
  341.7 4.7 multiply_convert_fusion.2
  346.7 28.4 %all-gather.11.cloned.1.call-done = bf16[2048,768]{1,0:T(8,128)(2,1)} async-done(((bf16[512,768]{1,0:T(8,128)(2,1)}), bf16[2048,768]{1,0:T(8,128)(2,1)}) %all-gather.11.cloned.1.call-update) | async-done | bytes 3145744 | tf_op jit(solution)/shard_map/all_gather | solution.py:224
  375.1 3.1 convolution_convert_fusion.1
  381.1 42.6 %while.29 = (s32[]{:T(128)}, f32[2,1024,3,64]{1,3,2,0:T(8,128)}, f32[2,1024,3,64]{1,3,2,0:T(8,128)}, bf16[2,1024,3,64]{1,3,2,0:T(8,128)(2,1)}, bf16[2,1024,3,64]...) while((s32[]{:T(128)}, f32[2,1024,3,64]{1,3,2,0:T(8,128)}, ...), condition=%wide.region_16.17_spmd.clone, body=%wide.region_14.16_spmd.sunk.clone | while | flops 2051404800 | bytes 124748936 | solution.py:231
  382.9 3.0 fusion.184
  386.0 3.1 multiply_reduce_fusion.15
  389.0 5.3 multiply_convert_fusion.5
  394.3 5.8 fusion.183
  404.1 3.0 fusion.184
  407.1 3.1 multiply_reduce_fusion.15
  410.2 5.3 multiply_convert_fusion.5
  415.5 5.8 fusion.183
  435.0 4.5 convolution_bitcast_fusion
  439.8 7.1 fusion.106
  446.9 4.2 fusion.105
  453.4 3.2 fusion.107
  457.3 22.2 %psum.93 = f32[768]{0:T(1024)} all-reduce(f32[768]{0:T(1024)S(1)} %copy-done.65), channel_id=1, replica_groups=mesh['dp'=8,'tensor'=4] {'dp'}, use_global_device_ids=true, to_apply=%region_34.35 | all-reduce | flops 768 | bytes 6144 | tf_op jit(solution)/shard_map/psum | solution.py:278
  479.6 18.5 %reduce-scatter.11.cloned.1.call-done = f32[512,768]{1,0:T(8,128)} async-done(((f32[2048,768]{1,0:T(8,128)}), f32[512,768]{1,0:T(8,128)}) %reduce-scatter.11.cloned.1.call-update) | async-done | bytes 1572880 | tf_op jit(solution)/shard_map/reduce_scatter | solution.py:247
  499.9 3.8 multiply_reduce_fusion.3
  508.6 3.2 fusion.100
  511.8 3.5 fusion.89
  517.6 6.6 psum.84
  524.2 2.9 select_reduce_fusion
  527.1 45.2 %all-reduce = (f32[768]{0:T(1024)}, f32[768]{0:T(1024)}, f32[768]{0:T(1024)}, f32[4608]{0:T(1024)}, f32[768]{0:T(1024)}) all-reduce(f32[768]{0:T(1024)S(1)} %get-tuple-element.175, f32[768]{0:T(1024)S(1)} %get-tuple-element.130, f32[768]{0:T(1024)S(1)} %copy-done.61, ...), channel_id=1, replica_groups=mesh['dp'=8,'tensor'=4] {'dp','tensor'}, use_global_device_ids=true, to_apply=%region_22.23 | all-reduce | flops 7680 | bytes 61440 | tf_op jit(solution)/shard_map/psum | solution.py:274
  572.4 2.8 broadcast_select_fusion
  575.1 165.3 %all-reduce.7.cloned.1.call-done = (f32[768,3,192]{0,2,1:T(8,128)}, f32[192,768]{1,0:T(8,128)}, f32[768,768]{1,0:T(8,128)}, f32[768,768]{1,0:T(8,128)}) async-done(((f32[768,3,192]{0,2,1:T(8,128)}, f32[192,768]{1,0:T(8,128)}, f32[768,768]{1,0:T(8,128)}, f32[768,768]{1,0:T(8,128)}), (f32[768,3,192]{0,2,1:T(8,128)}, f32[192,768]{1,0:T(8,128)}, f32[768,768]{1,0:T(8,128)}, ...) | async-done | bytes 7077904 | tf_op jit(solution)/shard_map/psum | solution.py:278
  740.4 140.9 %all-reduce.5.cloned.1.call-done = f32[128,4608]{1,0:T(8,128)} async-done(((f32[128,4608]{1,0:T(8,128)}), f32[128,4608]{1,0:T(8,128)}) %all-reduce.5.cloned.1.call-update) | async-done | bytes 2359312 | tf_op jit(solution)/shard_map/psum | solution.py:274
  881.4 3.4 copy.123
  (261 shorter events, 87.2 us)
Async XLA Ops:
  7.2 189.3 %copy-start = (bf16[768,768]{1,0:T(8,128)(2,1)S(1)}, bf16[768,768]{1,0:T(8,128)(2,1)}, u32[]{:S(2)}) copy-start(bf16[768,768]{1,0:T(8,128)(2,1)} %param.31) | copy-start | bytes 3538948
  7.2 5.5 copy-start.66
  7.2 5.5 copy-start.62
  7.2 5.5 copy-start.63
  7.2 5.5 copy-start.20
  7.2 47.1 %all-gather.5.cloned.1.call-start = ((), (), s32[]{:S(2)}) async-start(), calls=%async_computation.4 | async-start | bytes 3932160 | tf_op jit(solution)/shard_map/all_gather | solution.py:175
  7.3 10.0 %copy-start.44 = (s32[512]{0:T(512)}, s32[512]{0:T(512)S(1)}, u32[]{:S(2)}) copy-start(s32[512]{0:T(512)S(1)} %add_select_fusion) | copy-start | bytes 6148
  8.1 151.0 %copy-start.40 = (f32[768]{0:T(1024)}, f32[768]{0:T(1024)S(1)}, u32[]{:S(2)}) copy-start(f32[768]{0:T(1024)S(1)} %convert_element_type.91) | copy-start | bytes 9220
  9.6 149.6 %copy-start.58 = (pred[512]{0:T(512)(128)(4,1)}, pred[512]{0:T(512)(128)(4,1)S(1)}, u32[]{:S(2)}) copy-start(pred[512]{0:T(512)(128)(4,1)S(1)} %fusion.83) | copy-start | bytes 1540
  11.1 6.2 copy-start.50
  12.7 4.6 copy-start.56
  12.7 4.6 copy-start.48
  13.4 7.6 copy-start.6
  17.3 3.7 copy-start.3
  23.0 136.2 %reduce-scatter.5.cloned.1.call-start = ((), (), s32[]{:S(2)}) async-start(), calls=%async_computation.5 | async-start | bytes 7864320 | tf_op jit(solution)/shard_map/reduce_scatter | solution.py:189
  23.3 31.1 %copy-start.72 = (bf16[768,3,192]{0,2,1:T(8,128)(2,1)S(1)}, bf16[768,3,192]{0,2,1:T(8,128)(2,1)}, u32[]{:S(2)}) copy-start(bf16[768,3,192]{0,2,1:T(8,128)(2,1)} %param.29) | copy-start | bytes 2654212
  100.6 95.8 %all-gather.7.cloned.1.call-start = ((), (), s32[]{:S(2)}) async-start(), calls=%async_computation.6 | async-start | bytes 3932160 | tf_op jit(solution)/shard_map/all_gather | solution.py:196
  101.3 240.4 %copy-start.42 = (f32[768]{0:T(1024)}, f32[768]{0:T(1024)S(1)}, u32[]{:S(2)}) copy-start(f32[768]{0:T(1024)S(1)} %convert_element_type.102) | copy-start | bytes 9220
  161.5 6.3 copy-start.4
  161.5 180.2 %copy-start.46 = (f32[512]{0:T(512)}, f32[512]{0:T(512)S(1)}, u32[]{:S(2)}) copy-start(f32[512]{0:T(512)S(1)} %broadcast_multiply_fusion.6) | copy-start | bytes 6148
  163.2 178.5 %copy-start.52 = (f32[512]{0:T(512)}, f32[512]{0:T(512)S(1)}, u32[]{:S(2)}) copy-start(f32[512]{0:T(512)S(1)} %add_rsqrt_fusion) | copy-start | bytes 6148
  167.8 59.3 %all-gather.9.cloned.1.call-start = ((), (), s32[]{:S(2)}) async-start(), calls=%async_computation.8 | async-start | bytes 3932160 | tf_op jit(solution)/shard_map/all_gather | solution.py:209
  168.4 132.9 %reduce-scatter.9.cloned.1.call-start = ((), (), s32[]{:S(2)}) async-start(), calls=%async_computation.9 | async-start | bytes 7864320 | tf_op jit(solution)/shard_map/reduce_scatter | solution.py:215
  242.8 98.9 %reduce-scatter.7.cloned.1.call-start = ((), (), s32[]{:S(2)}) async-start(), calls=%async_computation.7 | async-start | bytes 3932160 | tf_op jit(solution)/shard_map/reduce_scatter | solution.py:203
  250.2 124.9 %all-gather.11.cloned.1.call-start = ((), (), s32[]{:S(2)}) async-start(), calls=%async_computation.10 | async-start | bytes 3932160 | tf_op jit(solution)/shard_map/all_gather | solution.py:224
  250.9 90.8 %copy-start.54 = (f32[768]{0:T(1024)}, f32[768]{0:T(1024)S(1)}, u32[]{:S(2)}) copy-start(f32[768]{0:T(1024)S(1)} %convert_element_type.108) | copy-start | bytes 9220
  341.7 33.4 %copy-start.34 = (bf16[192,768]{1,0:T(8,128)(2,1)S(1)}, bf16[192,768]{1,0:T(8,128)(2,1)}, u32[]{:S(2)}) copy-start(bf16[192,768]{1,0:T(8,128)(2,1)} %param.30) | copy-start | bytes 884740
  346.4 151.6 %reduce-scatter.11.cloned.1.call-start = ((), (), s32[]{:S(2)}) async-start(), calls=%async_computation.11 | async-start | bytes 7864320 | tf_op jit(solution)/shard_map/reduce_scatter | solution.py:247
  394.3 5.8 copy-start.2
  415.5 5.8 copy-start.2
  439.5 300.9 %all-reduce.7.cloned.1.call-start = ((), (), s32[]{:S(2)}) async-start(), calls=%async_computation.13 | async-start | bytes 14155776 | tf_op jit(solution)/shard_map/psum | solution.py:278
  439.8 7.1 copy-start.70
  439.8 7.1 copy-start.75
  446.9 4.2 copy-start.13
  446.9 4.2 copy-start.21
  446.9 5.8 copy-start.69
  456.6 424.7 %all-reduce.5.cloned.1.call-start = ((), (), s32[]{:S(2)}) async-start(), calls=%async_computation.12 | async-start | bytes 4718592 | tf_op jit(solution)/shard_map/psum | solution.py:274
  479.5 20.2 %copy-start.7 = (bf16[512,768]{1,0:T(8,128)(2,1)S(1)}, bf16[512,768]{1,0:T(8,128)(2,1)}, u32[]{:S(2)}) copy-start(bf16[512,768]{1,0:T(8,128)(2,1)} %param.20) | copy-start | bytes 2359300
  479.5 20.2 %copy-start.41 = (f32[768]{0:T(1024)S(1)}, f32[768]{0:T(1024)}, u32[]{:S(2)}) copy-start(f32[768]{0:T(1024)} %copy-done.40) | copy-start | bytes 9220
  479.5 20.2 %copy-start.49 = (f32[768]{0:T(1024)S(1)}, f32[768]{0:T(1024)}, u32[]{:S(2)}) copy-start(f32[768]{0:T(1024)} %copy-done.48) | copy-start | bytes 9220
  479.5 20.2 %copy-start.51 = (f32[512]{0:T(512)S(1)}, f32[512]{0:T(512)}, u32[]{:S(2)}) copy-start(f32[512]{0:T(512)} %copy-done.50) | copy-start | bytes 6148
  479.5 20.3 %copy-start.57 = (f32[512]{0:T(512)S(1)}, f32[512]{0:T(512)}, u32[]{:S(2)}) copy-start(f32[512]{0:T(512)} %copy-done.56) | copy-start | bytes 6148
  479.6 20.3 %copy-start.59 = (pred[512]{0:T(512)(128)(4,1)S(1)}, pred[512]{0:T(512)(128)(4,1)}, u32[]{:S(2)}) copy-start(pred[512]{0:T(512)(128)(4,1)} %copy-done.58) | copy-start | bytes 1540
  499.9 3.8 copy-start.9
  499.9 3.8 copy-start.17
  508.6 3.2 copy-start.64
  881.4 3.4 copy-start.31
  887.4 3.9 copy-start.1
  (44 other events, 74.4 us)
Sparse Core Ops, SparseCore 0:
  23.1 31.2 all-gather.4
  100.8 58.3 reduce-scatter.4
  167.9 28.5 all-gather.6
  198.6 28.5 all-gather.8
  242.9 58.3 reduce-scatter.8
  303.7 37.9 reduce-scatter.6
  346.6 28.5 all-gather.10
  439.6 58.3 reduce-scatter.10
  503.6 236.7 all-reduce.6
  747.3 134.0 all-reduce.4
where the time goes:
time: 905 us; the launch traced here: 899 us
  waiting for transfers between devices  572 us (63%)
  matrix products  117 us (13%)
  blocking collectives  74.1 us (8%)
  local copies, waits for them, and re-layouts  60.8 us (7%)
  other arithmetic  56.7 us (6%)
  between operations  15.5 us (2%)
    psum x1, waiting for transfers between devices, per_device(): lax.psum((grad_qkv, grad_out_weight, grad_up, grad_up_bias, grad_down), '...  165 us
    psum x1, waiting for transfers between devices, per_device(): lax.psum((grad_ada_weight, grad_ada_bias, grad_gain_one, grad_gain_two, g...  141 us
    reduce_scatter x1, waiting for transfers between devices, per_device(): lax.psum_scatter(partial_attn, 'tensor', scatter_dimension=0, tiled=True)  57.9 us
    reduce_scatter x1, waiting for transfers between devices, per_device(): lax.psum_scatter(contract_cols(grad_upper, up_weight), 'tensor', scatter_...  50.4 us
    psum x1, blocking collectives, per_device(): lax.psum((grad_ada_weight, grad_ada_bias, grad_gain_one, grad_gain_two, g...  45.2 us
    reduce_scatter x1, waiting for transfers between devices, per_device(): lax.psum_scatter(partial_mlp.astype(jnp.bfloat16), 'tensor', scatter_dime...  35.7 us
    unnamed x152, local copies, waits for them, and re-layouts  34.3 us
    all_gather x1, waiting for transfers between devices, per_device(): lax.all_gather(grad_branch_attn, 'tensor', axis=0, tiled=True)  28.4 us
  transfers between devices with their start and end apart: 10, of which 10 were waited for; matrix products, arithmetic and copies ran while one was open for 7% of the time, Pallas kernels for 0%

commit v1 on v0

v1 whole, which is shorter than its diff:
```python
import functools

import jax
import jax.numpy as jnp
import numpy as np
from jax import lax
from jax.experimental import pallas as pl
from jax.experimental.pallas import tpu as pltpu
from jax.sharding import PartitionSpec as P

BF = jnp.bfloat16
F = jnp.float32
HD = 64
LEN = 1024
EPS = 1e-05
GELU_COEF = 0.7978845608028654
CUBIC_COEF = 0.044715
SCALE = 0.125
LOG2E = 1.4426950408889634
EXP_SCALE = SCALE * LOG2E
MIB = 1 << 20


def nn(a, b):
    return lax.dot_general(a, b, (((1,), (0,)), ((), ())), preferred_element_type=F)


def nt(a, b):
    return lax.dot_general(a, b, (((1,), (1,)), ((), ())), preferred_element_type=F)


def tn(a, b):
    return lax.dot_general(a, b, (((0,), (0,)), ((), ())), preferred_element_type=F)


def matmul_high(left, right):
    return jnp.dot(left, right, precision=lax.Precision.HIGHEST, preferred_element_type=F)


def normalize(values):
    centered = values - jnp.mean(values, axis=-1, keepdims=True)
    inv = lax.rsqrt(jnp.mean(centered * centered, axis=-1, keepdims=True) + EPS)
    return centered * inv, inv


def layer_back(grad_norm, normed, inv):
    mean_grad = jnp.mean(grad_norm, axis=-1, keepdims=True)
    mean_cross = jnp.mean(grad_norm * normed, axis=-1, keepdims=True)
    return inv * (grad_norm - mean_grad - normed * mean_cross)


def halves_turned(v):
    parts = []
    for h in range(v.shape[1] // HD):
        lo = v[:, h * HD : h * HD + HD // 2]
        hi = v[:, h * HD + HD // 2 : (h + 1) * HD]
        parts += [-hi, lo]
    return jnp.concatenate(parts, axis=1)


def halves_back(v):
    parts = []
    for h in range(v.shape[1] // HD):
        lo = v[:, h * HD : h * HD + HD // 2]
        hi = v[:, h * HD + HD // 2 : (h + 1) * HD]
        parts += [hi, -lo]
    return jnp.concatenate(parts, axis=1)


def tables(block, heads):
    cos, sin = block[:, :HD], block[:, HD:]
    return jnp.concatenate([cos] * heads, axis=1), jnp.concatenate([sin] * heads, axis=1)


def call(kernel, outs, args, flops, grid=None, in_specs=None, out_specs=None, scratch=(), aliases=None, vmem=48, name=None):
    nbytes = sum(a.size * a.dtype.itemsize for a in args) + sum(o.size * o.dtype.itemsize for o in outs)
    kwargs = {}
    if grid is not None:
        kwargs["grid"] = grid
    if in_specs is None:
        in_specs = [pl.BlockSpec(memory_space=pltpu.VMEM)] * len(args)
    if out_specs is None:
        out_specs = [pl.BlockSpec(memory_space=pltpu.VMEM)] * len(outs)
    return pl.pallas_call(
        kernel,
        out_shape=tuple(outs),
        in_specs=in_specs,
        out_specs=tuple(out_specs),
        scratch_shapes=list(scratch),
        input_output_aliases=aliases or {},
        compiler_params=pltpu.CompilerParams(vmem_limit_bytes=vmem * MIB),
        cost_estimate=pl.CostEstimate(flops=flops, bytes_accessed=nbytes, transcendentals=0),
        name=name,
        **kwargs,
    )(*args)


def sds(shape, dtype):
    return jax.ShapeDtypeStruct(shape, dtype)


def head_kernel(tok, noised, cot, mask, gain, time, ada_w, ada_b, mod_o, h1_o, gm_o, gdb_o):
    d = tok.shape[1]
    tv = jnp.broadcast_to(time[...].astype(F), (16, time.shape[1]))
    s = tv / (1.0 + jnp.exp(-tv))
    hi = s.astype(BF).astype(F)
    mid = (s - hi).astype(BF).astype(F)
    low = (s - hi - mid).astype(BF).astype(F)
    stacked = jnp.concatenate([hi, mid, low], axis=0).astype(BF)
    for i in range(6):
        cols = pl.ds(i * d, d)
        m = nn(stacked, ada_w[:, cols])
        m = m[0:1] + m[16:17] + m[32:33] + ada_b[:, cols].astype(F)
        mod_o[i : i + 1, :] = m
    inputs = jnp.where(noised[...] > 0.5, mask[...].astype(F), tok[...].astype(F))
    n1, _ = normalize(inputs)
    h1 = n1 * gain[...].astype(F) * (1.0 + mod_o[1:2, :]) + mod_o[0:1, :]
    h1_o[...] = h1.astype(BF)
    gm = (mod_o[5:6, :] * cot[...].astype(F)).astype(BF)
    gm_o[...] = gm
    gdb_o[...] = jnp.sum(gm.astype(F), axis=0, keepdims=True)


def attn_kernel(h1o, h1p, wt, cs, q_o, k_o, v_o, att_o, st_o, qm, st):
    rows = h1o.shape[0]
    width = q_o.shape[1]
    heads = width // HD
    cos, sin = tables(cs[0:rows, :], heads)
    q = nt(h1o[...], wt[0:width, :])
    q = (q * cos + halves_turned(q) * sin).astype(BF)
    q_o[...] = q
    qf = q.astype(F)
    lane_q = lax.broadcasted_iota(jnp.int32, (rows, width), 1) // HD
    for h in range(heads):
        qm[h] = jnp.where(lane_q == h, qf, 0.0).astype(BF)
    k = nt(h1o[...], wt[width : 2 * width, :])
    k_o[0:rows, :] = (k * cos + halves_turned(k) * sin).astype(BF)
    v_o[0:rows, :] = nt(h1o[...], wt[2 * width : 3 * width, :]).astype(BF)
    cos, sin = tables(cs[rows : 2 * rows, :], heads)
    k = nt(h1p[...], wt[width : 2 * width, :])
    k_o[rows : 2 * rows, :] = (k * cos + halves_turned(k) * sin).astype(BF)
    v_o[rows : 2 * rows, :] = nt(h1p[...], wt[2 * width : 3 * width, :]).astype(BF)
    tile = 256
    lane = lax.broadcasted_iota(jnp.int32, (tile, width), 1) // HD
    lane_s = lax.broadcasted_iota(jnp.int32, (tile, 128), 1)

    def body(i, carry):
        rs = pl.ds(pl.multiple_of(i * tile, tile), tile)
        acc = jnp.zeros((tile, width), F)
        stats = jnp.zeros((tile, 128), F)
        for h in range(heads):
            s = nt(qm[h, rs, :], k_o[...])
            m = jnp.max(s, axis=1, keepdims=True)
            e = jnp.exp2((s - m) * EXP_SCALE)
            total = jnp.sum(e, axis=1, keepdims=True)
            p = (e * (1.0 / total)).astype(BF)
            o = nn(p, v_o[...])
            acc = jnp.where(lane == h, o, acc)
            stats = jnp.where(lane_s == h, m * EXP_SCALE + jnp.log2(total), stats)
        att_o[rs, :] = acc.astype(BF)
        st[rs, :] = stats
        return carry

    lax.fori_loop(0, rows // tile, body, 0)
    st_o[...] = st[...].T[0:8, :]


def mid_kernel(a0, a1, a2, a3, w0, w1, w2, w3, tok, noised, mask, gain, mod, branch_o, mixed_o, h2_o):
    branch = nn(a0[...], w0[...]) + nn(a1[...], w1[...]) + nn(a2[...], w2[...]) + nn(a3[...], w3[...])
    inputs = jnp.where(noised[...] > 0.5, mask[...].astype(F), tok[...].astype(F))
    mixed = inputs + mod[2:3, :] * branch
    n2, _ = normalize(mixed)
    h2 = n2 * gain[...].astype(F) * (1.0 + mod[4:5, :]) + mod[3:4, :]
    branch_o[...] = branch
    mixed_o[...] = mixed
    h2_o[...] = h2.astype(BF)


def mlp_kernel(has_acc, has_add, h2, gm, wu, bu, wd, *refs):
    refs = list(refs)
    if has_acc:
        bin_, gin = refs[0], refs[1]
        refs = refs[2:]
    if has_add:
        dda, dua = refs[0], refs[1]
        refs = refs[2:]
    b_o, g_o, dd_o, du_o, gub_o = refs
    u = nn(h2[...], wu[...]) + bu[...].astype(F)
    th = jnp.tanh(GELU_COEF * (u + CUBIC_COEF * u * u * u))
    act = (0.5 * u * (1.0 + th)).astype(BF)
    slope = 0.5 * (1.0 + th) + 0.5 * u * (1.0 - th * th) * GELU_COEF * (1.0 + 3.0 * CUBIC_COEF * u * u)
    ga = nt(gm[...], wd[...])
    gu_f = (ga * slope).astype(BF).astype(F)
    gu = gu_f.astype(BF)
    gub_o[...] = jnp.sum(gu_f, axis=0, keepdims=True)
    b_new = nn(act, wd[...])
    g_new = nt(gu, wu[...])
    first = pl.program_id(0) == 0

    @pl.when(first)
    def _():
        if has_acc:
            b_o[...] = bin_[...] + b_new
            g_o[...] = gin[...] + g_new
        else:
            b_o[...] = b_new
            g_o[...] = g_new

    @pl.when(jnp.logical_not(first))
    def _():
        b_o[...] += b_new
        g_o[...] += g_new

    dd = tn(act, gm[...])
    du = tn(h2[...], gu)
    if has_add:
        dd = dd + dda[...].astype(F)
        du = du + dua[...].astype(F)
    dd_o[...] = dd.astype(dd_o.dtype)
    du_o[...] = du.astype(du_o.dtype)


def mlp_part(h2, gm, wu, bu, wd, acc, add, dtype, name):
    rows, d = h2.shape
    hidden = wu.shape[1]
    hc = 256
    const = lambda i: (0, 0)
    full = pl.BlockSpec((rows, d), const)
    up = pl.BlockSpec((d, hc), lambda i: (0, i))
    down = pl.BlockSpec((hc, d), lambda i: (i, 0))
    vec = pl.BlockSpec((1, hc), lambda i: (0, i))
    args = [h2, gm, wu, bu, wd]
    specs = [full, full, up, vec, down]
    aliases = {}
    if acc is not None:
        aliases = {5: 0, 6: 1}
        args += list(acc)
        specs += [full, full]
    if add is not None:
        args += list(add)
        specs += [down, up]
    return call(
        functools.partial(mlp_kernel, acc is not None, add is not None),
        [sds((rows, d), F), sds((rows, d), F), sds((hidden, d), dtype), sds((d, hidden), dtype), sds((1, hidden), F)],
        args,
        12 * rows * d * hidden,
        grid=(hidden // hc,),
        in_specs=specs,
        out_specs=[full, full, down, up, vec],
        aliases=aliases,
        name=name,
    )


def post_kernel(bm, gh, mixed, cot, branch, a0, a1, a2, a3, w0, w1, w2, w3, gain, mod, db, out_o, gmix_o, ga0, ga1, ga2, ga3, dw_o, sums_o):
    n2, inv = normalize(mixed[...])
    gain2 = gain[...].astype(F)
    scale1 = 1.0 + mod[4:5, :]
    c = cot[...].astype(F)
    bmlp = bm[...] + db[...].astype(F)
    out_o[...] = (mixed[...] + mod[5:6, :] * bmlp).astype(BF)
    g = gh[...]
    gs = g * scale1
    grad_mixed = c + layer_back(gs * gain2, n2, inv)
    gmix_o[...] = grad_mixed
    rows = [
        jnp.sum(gs * n2, axis=0, keepdims=True),
        jnp.sum(grad_mixed * branch[...], axis=0, keepdims=True),
        jnp.sum(g, axis=0, keepdims=True),
        jnp.sum(g * n2 * gain2, axis=0, keepdims=True),
        jnp.sum(c * bmlp, axis=0, keepdims=True),
    ]
    sums = jnp.concatenate(rows + [jnp.zeros((3, g.shape[1]), F)], axis=0)
    gba = (mod[2:3, :] * grad_mixed).astype(BF)
    wide = a0.shape[1]
    first = pl.program_id(0) == 0
    for r, (a, w, ga) in enumerate(((a0, w0, ga0), (a1, w1, ga1), (a2, w2, ga2), (a3, w3, ga3))):
        ga[...] = nt(gba, w[...]).astype(BF)
        dw = tn(a[...], gba)
        place = pl.ds(r * wide, wide)

        @pl.when(first)
        def _():
            dw_o[place, :] = dw

        @pl.when(jnp.logical_not(first))
        def _():
            dw_o[place, :] += dw

    @pl.when(first)
    def _():
        sums_o[...] = sums

    @pl.when(jnp.logical_not(first))
    def _():
        sums_o[...] += sums


def back_kernel(q, k, v, go, st, cs, dq_o, own_o, par_o, dk, dv, km, dq):
    rows, width = q.shape
    heads = width // HD
    keys = k.shape[0]
    kf = k[...].astype(F)
    lane_k = lax.broadcasted_iota(jnp.int32, (keys, width), 1) // HD
    for h in range(heads):
        km[h] = jnp.where(lane_k == h, kf, 0.0).astype(BF)
    dk[...] = jnp.zeros_like(dk)
    dv[...] = jnp.zeros_like(dv)
    tile = 256
    lane = lax.broadcasted_iota(jnp.int32, (tile, width), 1) // HD

    def body(i, carry):
        rs = pl.ds(pl.multiple_of(i * tile, tile), tile)
        qt = q[rs, :].astype(F)
        gt = go[rs, :].astype(F)
        acc = jnp.zeros((tile, width), F)
        for h in range(heads):
            qm = jnp.where(lane == h, qt, 0.0).astype(BF)
            gm = jnp.where(lane == h, gt, 0.0).astype(BF)
            s = nt(k[...], qm)
            p = jnp.exp2(s * EXP_SCALE - st[h : h + 1, rs])
            dp = nt(v[...], gm)
            inner = jnp.sum(p * dp, axis=0, keepdims=True)
            ds = (p * (dp - inner)).astype(BF)
            dv[...] += nn(p.astype(BF), gm)
            dk[...] += nn(ds, qm)
            acc = acc + tn(ds, km[h])
        dq[rs, :] = acc
        return carry

    lax.fori_loop(0, rows // tile, body, 0)
    cos, sin = tables(cs[...], heads)
    g = dq[...] * SCALE
    dq_o[...] = (g * cos + halves_back(g * sin)).astype(BF)
    own_o[...] = jnp.concatenate([dk[0:rows, :] * SCALE, dv[0:rows, :]], axis=1)
    par_o[...] = jnp.concatenate([dk[rows : 2 * rows, :] * SCALE, dv[rows : 2 * rows, :]], axis=1)


def proj_kernel(has_acc, has_add, dq, own, rcv, cs, h1, wt, *refs):
    refs = list(refs)
    if has_acc:
        gin = refs.pop(0)
    if has_add:
        dwa = refs.pop(0)
    g_o, dw_o = refs
    width = dq.shape[1]
    cos, sin = tables(cs[...], width // HD)
    gkv = own[...] + rcv[...]
    gk = gkv[:, :width]
    gk = (gk * cos + halves_back(gk * sin)).astype(BF)
    gv = gkv[:, width:].astype(BF)
    parts = (dq[...], gk, gv)
    g = gin[...] if has_acc else 0.0
    for i, part in enumerate(parts):
        place = slice(i * width, (i + 1) * width)
        g = g + nn(part, wt[place, :])
        dw = tn(part, h1[...])
        if has_add:
            dw = dw + dwa[place, :].astype(F)
        dw_o[place, :] = dw.astype(dw_o.dtype)
    g_o[...] = g


def tail_kernel(gh, gmix, tok, noised, mask, gain, mod, gt_o, sums_o):
    mask_on = noised[...] > 0.5
    inputs = jnp.where(mask_on, mask[...].astype(F), tok[...].astype(F))
    n1, inv = normalize(inputs)
    gain1 = gain[...].astype(F)
    g = gh[...]
    gs = g * (1.0 + mod[1:2, :])
    gi = gmix[...] + layer_back(gs * gain1, n1, inv)
    gt_o[...] = jnp.where(mask_on, 0.0, gi)
    rows = [
        jnp.sum(gs * n1, axis=0, keepdims=True),
        jnp.sum(jnp.where(mask_on, gi, 0.0), axis=0, keepdims=True),
        jnp.sum(g, axis=0, keepdims=True),
        jnp.sum(g * n1 * gain1, axis=0, keepdims=True),
    ]
    sums_o[...] = jnp.concatenate(rows + [jnp.zeros((4, g.shape[1]), F)], axis=0)


def swap(value, axis, bit):
    return lax.ppermute(value, axis, [(i, i ^ bit) for i in range(lax.axis_size(axis))])


def bit_of(index, bit):
    return (index // bit) % 2


def joined(mine, other, bit, axis=0):
    return jnp.where(bit == 0, jnp.concatenate([mine, other], axis), jnp.concatenate([other, mine], axis))


def reduce_dp(total, dp, n_dp):
    rows = total.shape[0]
    bits = []
    step = 1
    while step < n_dp:
        bits.append(step)
        step *= 2
    halved = bits[:3]
    for b in halved:
        rows //= 2
        mine = bit_of(dp, b)
        keep = lax.dynamic_slice_in_dim(total, mine * rows, rows, 0)
        send = lax.dynamic_slice_in_dim(total, (1 - mine) * rows, rows, 0).astype(BF)
        total = keep + swap(send, "dp", b).astype(F)
    for b in bits[3:]:
        total = total + swap(total, "dp", b)
    out = total.astype(BF)
    for b in reversed(halved):
        out = joined(out, swap(out, "dp", b), bit_of(dp, b))
    return out.astype(F)


def rotary_block():
    freq = np.float32(10000.0) ** (np.float32(-2.0) * np.arange(HD // 2, dtype=np.float32) / np.float32(HD))
    angle = np.arange(LEN, dtype=np.float32)[:, None] * freq[None, :].astype(np.float32)
    angle = np.concatenate([angle, angle], axis=1)
    return np.concatenate([np.cos(angle), np.sin(angle)], axis=1).astype(np.float32)


def per_device(tokens, time_emb, prefix_len, noise_mask, mask_embed, gain_attn, gain_mlp, ada_weight, ada_bias, qkv_weight, out_weight, up_weight, up_bias, down_weight, down_bias, cotangent):
    rows, d = tokens.shape
    n_dp = lax.axis_size("dp")
    assert lax.axis_size("tensor") == 4 and time_emb.shape[0] == 2 and 2 * rows == LEN
    t = lax.axis_index("tensor")
    dp = lax.axis_index("dp")
    xb, cb = t // 2, t % 2
    width = qkv_weight.shape[2]

    wt = qkv_weight.transpose(1, 2, 0).reshape(3 * width, d)
    bu = up_bias.reshape(1, -1)
    own = (wt, out_weight, up_weight, down_weight, bu)
    near = tuple(swap(w, "tensor", 1) for w in own)
    far = tuple(swap(w, "tensor", 2) for w in own)
    far_near = tuple(swap(w, "tensor", 1) for w in far)
    wts, wos, wus, wds, bus = zip(own, near, far, far_near)

    position = cb * rows + jnp.arange(rows, dtype=jnp.int32)
    prefix = lax.dynamic_slice_in_dim(prefix_len, xb, 1, 0)
    noised = ((noise_mask == 1) & (position >= prefix)).astype(F).reshape(rows, 1)
    time_row = lax.dynamic_slice_in_dim(time_emb, xb, 1, 0)
    table = jnp.asarray(rotary_block())
    cs = jnp.where(cb == 0, table, jnp.concatenate([table[rows:], table[:rows]], axis=0))
    cs_own = cs[:rows]
    vec = lambda v: v.reshape(1, -1)
    mask, gain1, gain2, db = vec(mask_embed), vec(gain_attn), vec(gain_mlp), vec(down_bias)

    mod, h1, gm, g_db = call(
        head_kernel,
        [sds((6, d), F), sds((rows, d), BF), sds((rows, d), BF), sds((1, d), F)],
        [tokens, noised, cotangent, mask, gain1, time_row, ada_weight, vec(ada_bias)],
        2 * 48 * 128 * 6 * d,
        name="head",
    )
    h1p = swap(h1, "tensor", 1)

    fwd = []
    for r in range(4):
        fwd.append(
            call(
                attn_kernel,
                [sds((rows, width), BF), sds((2 * rows, width), BF), sds((2 * rows, width), BF), sds((rows, width), BF), sds((8, rows), F)],
                [h1, h1p, wts[r], cs],
                2 * rows * d * width * 5 + 4 * rows * 2 * rows * 256 * 3,
                scratch=[pltpu.VMEM((width // HD, rows, width), BF), pltpu.VMEM((rows, 128), F)],
                name=f"attn{r}",
            )
        )
    atts = [f[3] for f in fwd]

    tile = 256
    tiled = lambda w: pl.BlockSpec((tile, w), lambda i: (i, 0))
    fixed = lambda a: pl.BlockSpec(a.shape, lambda i: (0, 0))
    branch, mixed, h2 = call(
        mid_kernel,
        [sds((rows, d), F), sds((rows, d), F), sds((rows, d), BF)],
        atts + list(wos) + [tokens, noised, mask, gain2, mod],
        2 * rows * d * 4 * width,
        grid=(rows // tile,),
        in_specs=[tiled(width)] * 4 + [fixed(w) for w in wos] + [tiled(d), tiled(1), fixed(mask), fixed(gain2), fixed(mod)],
        out_specs=[tiled(d)] * 3,
        name="mid",
    )

    b1, g1, dd1, du1, gub1 = mlp_part(h2, gm, wus[1], bus[1], wds[1], None, None, BF, "mlp1")
    add0 = (swap(dd1, "tensor", 1), swap(du1, "tensor", 1))
    b3, g3, dd3, du3, gub3 = mlp_part(h2, gm, wus[3], bus[3], wds[3], (b1, g1), None, BF, "mlp3")
    add2 = (swap(dd3, "tensor", 1), swap(du3, "tensor", 1))
    b2, g2, dd2, du2, gub2 = mlp_part(h2, gm, wus[2], bus[2], wds[2], (b3, g3), add2, BF, "mlp2")
    b0, g0, dd0, du0, gub0 = mlp_part(h2, gm, wus[0], bus[0], wds[0], (b2, g2), add0, F, "mlp0")
    down_total = dd0 + swap(dd2, "tensor", 2).astype(F)
    up_total = du0 + swap(du2, "tensor", 2).astype(F)
    grad_down = reduce_dp(down_total, dp, n_dp)
    grad_up = reduce_dp(up_total, dp, n_dp)

    post = call(
        post_kernel,
        [sds((rows, d), BF), sds((rows, d), F)] + [sds((rows, width), BF)] * 4 + [sds((4 * width, d), F), sds((8, d), F)],
        [b0, g0, mixed, cotangent, branch] + atts + list(wos) + [gain2, mod, db],
        4 * rows * d * 4 * width,
        grid=(rows // tile,),
        in_specs=[tiled(d)] * 5 + [tiled(width)] * 4 + [fixed(w) for w in wos] + [fixed(gain2), fixed(mod), fixed(db)],
        out_specs=[tiled(d)] * 2 + [tiled(width)] * 4 + [pl.BlockSpec((4 * width, d), lambda i: (0, 0)), pl.BlockSpec((8, d), lambda i: (0, 0))],
        name="post",
    )
    output, grad_mixed = post[0], post[1]
    g_att = post[2:6]
    dwo, sums_two = post[6], post[7]
    part = lambda r: dwo[r * width : (r + 1) * width]
    o1 = swap(part(1).astype(BF), "tensor", 1)
    o3 = swap(part(3).astype(BF), "tensor", 1)
    o2 = swap((part(2) + o3.astype(F)).astype(BF), "tensor", 2)
    grad_out = reduce_dp(part(0) + o1.astype(F) + o2.astype(F), dp, n_dp)

    gh1 = None
    dws = {}
    for pair in ((3, 2), (1, 0)):
        backs = {}
        for r in pair:
            q, k, v, _, st = fwd[r]
            backs[r] = call(
                back_kernel,
                [sds((rows, width), BF), sds((rows, 2 * width), F), sds((rows, 2 * width), F)],
                [q, k, v, g_att[r], st, cs_own],
                10 * rows * 2 * rows * 256 * 3,
                scratch=[pltpu.VMEM((2 * rows, width), F), pltpu.VMEM((2 * rows, width), F), pltpu.VMEM((width // HD, 2 * rows, width), BF), pltpu.VMEM((rows, width), F)],
                name=f"back{r}",
            )
        for r in pair:
            dq, own_kv, _ = backs[r]
            rcv_kv = swap(backs[r ^ 1][2], "tensor", 1)
            args = [dq, own_kv, rcv_kv, cs_own, h1, wts[r]]
            aliases = {}
            if gh1 is not None:
                aliases = {len(args): 0}
                args.append(gh1)
            add = {2: 3, 0: 1}.get(r)
            if add is not None:
                args.append(swap(dws[add], "tensor", 1))
            gh1, dws[r] = call(
                functools.partial(proj_kernel, gh1 is not None, add is not None),
                [sds((rows, d), F), sds((3 * width, d), F if r == 0 else BF)],
                args,
                4 * rows * d * 3 * width,
                aliases=aliases,
                name=f"proj{r}",
            )
    qkv_total = dws[0] + swap(dws[2], "tensor", 2).astype(F)
    grad_qkv = reduce_dp(qkv_total, dp, n_dp).reshape(3, width, d).transpose(2, 0, 1)

    grad_tokens, sums_one = call(
        tail_kernel,
        [sds((rows, d), F), sds((8, d), F)],
        [gh1, grad_mixed, tokens, noised, mask, gain1, mod],
        10 * rows * d,
        name="tail",
    )

    hid = jnp.concatenate([gub0, gub1, gub2, gub3], axis=0)
    mods = jnp.concatenate([sums_one[2:4], sums_two[1:5]], axis=0)
    shared = jnp.concatenate([sums_one[0:2], sums_two[0:1], g_db], axis=0)
    got = swap(jnp.concatenate([hid[1:2], hid[3:4], shared, mods], axis=0), "tensor", 1)
    hid = hid[0::2] + got[0:2]
    shared = shared + got[2:6]
    mods = mods + got[6:]
    got = swap(jnp.concatenate([hid[1:2], shared, mods], axis=0), "tensor", 2)
    shared = jnp.concatenate([hid[0:1] + got[0:1], shared + got[1:5]], axis=0)
    mods = joined(mods[None], got[5:][None], xb)
    pair_mods = mods.reshape(2, 6 * d)
    times = time_emb
    step = 1
    while step < n_dp:
        got = swap(jnp.concatenate([shared, mods.reshape(-1, d)], axis=0), "dp", step)
        shared = shared + got[0:5]
        mods = joined(mods, got[5:].reshape(mods.shape), bit_of(dp, step))
        times = joined(times, swap(times, "dp", step), bit_of(dp, step))
        step *= 2
    mods = mods.reshape(-1, 6 * d)
    ada_full = ada_weight.astype(F)
    tv = time_emb.astype(F)
    sig = jax.nn.sigmoid(tv)
    grad_time = matmul_high(pair_mods, ada_full.T) * sig * (1.0 + tv * (1.0 - sig))
    silu = jax.nn.silu(times.astype(F))
    grad_ada_weight = lax.dot_general(silu, mods, (((0,), (0,)), ((), ())), precision=lax.Precision.HIGHEST, preferred_element_type=F)
    grad_ada_bias = jnp.sum(mods, axis=0)
    return (
        output,
        grad_tokens,
        grad_time,
        shared[2],
        shared[1],
        shared[3],
        grad_ada_weight,
        grad_ada_bias,
        grad_qkv,
        grad_out,
        grad_up,
        shared[0],
        grad_down,
        shared[4],
    )


def solution(mesh):
    group = ("dp", "tensor")
    in_specs = (P(group, None), P("dp", None), P("dp"), P(group), P(), P(), P(), P(), P(), P(None, None, "tensor"), P("tensor", None), P(None, "tensor"), P("tensor"), P("tensor", None), P(), P(group, None))
    out_specs = (P(group, None), P(group, None), P("dp", None), P(), P(), P(), P(), P(), P(None, None, "tensor"), P("tensor", None), P(None, "tensor"), P("tensor"), P("tensor", None), P())
    return jax.shard_map(per_device, mesh=mesh, in_specs=in_specs, out_specs=out_specs, check_vma=False)
```

time: 905 us -> 456 us (0.50)
  waiting for transfers between devices: 572 us -> 197 us
  Pallas kernels: 0 us -> 119 us
  matrix products: 117 us -> 5.95 us
  blocking collectives: 74.1 us -> 0 us
  starting transfers between devices: 1.51 us -> 44.7 us
  other arithmetic: 56.7 us -> 31.9 us
  between operations: 15.5 us -> 2.58 us
  local copies, waits for them, and re-layouts: 60.8 us -> 50.1 us
    psum x2 -> x0, waiting for transfers between devices: 306 us -> none  [the longest x1 165 us: per_device(): lax.psum((grad_qkv, grad_out_weight, grad_up, grad_up_bias, grad_down), '...]
    ppermute x0 -> x64, waiting for transfers between devices: none -> 197 us  [swap(): lax.ppermute(value, axis, [(i, i ^ bit) for i in range(lax.axis_size(axis...]
    reduce_scatter x4 -> x0, waiting for transfers between devices: 162 us -> none  [the longest x1 57.9 us: per_device(): lax.psum_scatter(partial_attn, 'tensor', scatter_dimension=0, tiled=True)]
    pallas_call x0 -> x20, Pallas kernels: none -> 119 us  [call(): pl.pallas_call(kernel, out_shape=tuple(outs), in_specs=in_specs, out_spec...]
    all_gather x4 -> x0, waiting for transfers between devices: 103 us -> none  [the longest x1 28.4 us: per_device(): lax.all_gather(grad_branch_attn, 'tensor', axis=0, tiled=True)]
    dot_general x26 -> x1, matrix products: 101 us -> 3.46 us  [per_device(): lax.dot_general(silu, mods, (((0,), (0,)), ((), ())), precision=lax.Preci...]
    psum x3 -> x0, blocking collectives: 74.1 us -> none  [the longest x1 45.2 us: per_device(): lax.psum((grad_ada_weight, grad_ada_bias, grad_gain_one, grad_gain_two, g...]
    ppermute x0 -> x64, starting transfers between devices: none -> 44.7 us  [swap(): lax.ppermute(value, axis, [(i, i ^ bit) for i in range(lax.axis_size(axis...]
  transfers between devices with their start and end apart: 10 -> 64, of which waited for: 10 -> 23; matrix products, arithmetic and copies ran while one was open for 7% -> 11% of each run, Pallas kernels for 0% -> 24%
where the time goes in v1:
time: 456 us; the launch traced here: 451 us
  waiting for transfers between devices  197 us (43%)
  Pallas kernels  119 us (26%)
  local copies, waits for them, and re-layouts  50.1 us (11%)
  starting transfers between devices  44.7 us (10%)
  other arithmetic  31.9 us (7%)
  matrix products  5.95 us (1%)
    ppermute x64, waiting for transfers between devices, swap(): lax.ppermute(value, axis, [(i, i ^ bit) for i in range(lax.axis_size(axis...  197 us
    pallas_call x20, Pallas kernels, call(): pl.pallas_call(kernel, out_shape=tuple(outs), in_specs=in_specs, out_spec...  119 us
    ppermute x64, starting transfers between devices, swap(): lax.ppermute(value, axis, [(i, i ^ bit) for i in range(lax.axis_size(axis...  44.7 us
    unnamed x224, local copies, waits for them, and re-layouts  37.6 us
  transfers between devices with their start and end apart: 64, of which 23 were waited for; matrix products, arithmetic and copies ran while one was open for 11% of the time, Pallas kernels for 24%

profile of v1, /device:TPU:0, one launch (start us, length us, event | category | flops | bytes accessed | tf_op | source)
XLA Modules:
  0.0 450.9 jit_solution(1510220401890372826)
XLA Ops:
  0.6 3.0 collective-permute-start.5
  19.9 10.9 %collective-permute-done.2.wt = bf16[576,768]{1,0:T(8,128)(2,1)} collective-permute-done((bf16[576,768]{1,0:T(8,128)(2,1)}, bf16[576,768]{1,0:T(8,128)(2,1)}, u32[]{:S(2)}, u32[]{:S(2)}) %collective-permute-start.2) | collective-permute-done | bytes 884768 | tf_op jit(solution)/shard_map/ppermute | solution.py:383
  32.8 23.2 %collective-permute-done.7.wu = bf16[768,768]{1,0:T(8,128)(2,1)} collective-permute-done((bf16[768,768]{1,0:T(8,128)(2,1)}, bf16[768,768]{1,0:T(8,128)(2,1)}, u32[]{:S(2)}, u32[]{:S(2)}) %collective-permute-start.7) | collective-permute-done | bytes 1179680 | tf_op jit(solution)/shard_map/ppermute | solution.py:383
  56.0 24.4 %collective-permute-done.9.wd = bf16[768,768]{1,0:T(8,128)(2,1)} collective-permute-done((bf16[768,768]{1,0:T(8,128)(2,1)}, bf16[768,768]{1,0:T(8,128)(2,1)}, u32[]{:S(2)}, u32[]{:S(2)}) %collective-permute-start.9) | collective-permute-done | bytes 1179680 | tf_op jit(solution)/shard_map/ppermute | solution.py:383
  81.7 5.2 %attn0.1 = (bf16[512,192]{1,0:T(8,128)(2,1)S(1)}, bf16[1024,192]{1,0:T(8,128)(2,1)S(1)}, bf16[1024,192]{1,0:T(8,128)(2,1)S(1)}, bf16[512,192]{1,0:T(8,128)(2,1)S(1)}, f32[8,512]{1,0:T(8,128)S(1)}) custom-call(bf16[512,768]{1,0:T(8,128)(2,1)S(1)} %get-tuple-element.91.h1o.h1, bf16[512,768]{1,0:T(8,128)(2,1)S(1)} %collective-permute-done.h1p, ...), custom_call_target="tpu_custom_call" | custom-call | flops 2365587456 | bytes 4177920 | tf_op jit(solution)/shard_map/attn0/pallas_call | solution.py:84
  89.8 6.3 %attn2.1 = (bf16[512,192]{1,0:T(8,128)(2,1)S(1)}, bf16[1024,192]{1,0:T(8,128)(2,1)S(1)}, bf16[1024,192]{1,0:T(8,128)(2,1)S(1)}, bf16[512,192]{1,0:T(8,128)(2,1)S(1)}, f32[8,512]{1,0:T(8,128)S(1)}) custom-call(bf16[512,768]{1,0:T(8,128)(2,1)S(1)} %get-tuple-element.91.h1o.h1, bf16[512,768]{1,0:T(8,128)(2,1)S(1)} %collective-permute-done.h1p, ...), custom_call_target="tpu_custom_call" | custom-call | flops 2365587456 | bytes 4177920 | tf_op jit(solution)/shard_map/attn2/pallas_call | solution.py:84
  99.6 5.0 %attn1.1 = (bf16[512,192]{1,0:T(8,128)(2,1)S(1)}, bf16[1024,192]{1,0:T(8,128)(2,1)S(1)}, bf16[1024,192]{1,0:T(8,128)(2,1)S(1)}, bf16[512,192]{1,0:T(8,128)(2,1)S(1)}, f32[8,512]{1,0:T(8,128)S(1)}) custom-call(bf16[512,768]{1,0:T(8,128)(2,1)S(1)} %get-tuple-element.91.h1o.h1, bf16[512,768]{1,0:T(8,128)(2,1)S(1)} %collective-permute-done.h1p, ...), custom_call_target="tpu_custom_call" | custom-call | flops 2365587456 | bytes 4177920 | tf_op jit(solution)/shard_map/attn1/pallas_call | solution.py:84
  109.6 6.5 %attn3.1 = (bf16[512,192]{1,0:T(8,128)(2,1)S(1)}, bf16[1024,192]{1,0:T(8,128)(2,1)S(1)}, bf16[1024,192]{1,0:T(8,128)(2,1)S(1)}, bf16[512,192]{1,0:T(8,128)(2,1)S(1)}, f32[8,512]{1,0:T(8,128)S(1)}) custom-call(bf16[512,768]{1,0:T(8,128)(2,1)S(1)} %get-tuple-element.91.h1o.h1, bf16[512,768]{1,0:T(8,128)(2,1)S(1)} %copy-done.52, ...), custom_call_target="tpu_custom_call" | custom-call | flops 2365587456 | bytes 4177920 | tf_op jit(solution)/shard_map/attn3/pallas_call | solution.py:84
  120.0 2.5 mid.1
  124.8 9.3 %mlp1.1 = (f32[512,768]{1,0:T(8,128)}, f32[512,768]{1,0:T(8,128)}, bf16[768,768]{1,0:T(8,128)(2,1)}, bf16[768,768]{1,0:T(8,128)(2,1)}, f32[1,768]{1,0:T(1,128)S(1)}) custom-call(bf16[512,768]{1,0:T(8,128)(2,1)S(1)} %get-tuple-element.97.h2, bf16[512,768]{1,0:T(8,128)(2,1)S(1)} %copy-done.46, bf16[768,768]{1,0:T(8,128)(2,1)S(1)} %collective-permute-done.13.wu, ...), custom_call_target="tpu_custom_call" | custom-call | flops 3623878656 | bytes 9441792 | tf_op jit(solution)/shard_map/mlp1/pallas_call | solution.py:84
  135.7 10.1 %mlp3.1 = (f32[512,768]{1,0:T(8,128)}, f32[512,768]{1,0:T(8,128)}, bf16[768,768]{1,0:T(8,128)(2,1)}, bf16[768,768]{1,0:T(8,128)(2,1)}, f32[1,768]{1,0:T(1,128)S(1)}) custom-call(bf16[512,768]{1,0:T(8,128)(2,1)S(1)} %get-tuple-element.97.h2, bf16[512,768]{1,0:T(8,128)(2,1)S(1)} %copy-done.46, ...), custom_call_target="tpu_custom_call", output_to_operand_aliasing={{0}: (5, {}), {1}: (6, {})} | custom-call | flops 3623878656 | bytes 12587520 | tf_op jit(solution)/shard_map/mlp3/pallas_call | solution.py:84
  154.2 10.8 %mlp2.1 = (f32[512,768]{1,0:T(8,128)}, f32[512,768]{1,0:T(8,128)}, bf16[768,768]{1,0:T(8,128)(2,1)S(1)}, bf16[768,768]{1,0:T(8,128)(2,1)S(1)}, f32[1,768]{1,0:T(1,128)S(1)}) custom-call(bf16[512,768]{1,0:T(8,128)(2,1)S(1)} %copy-done.50, bf16[512,768]{1,0:T(8,128)(2,1)S(1)} %copy-done.47, ...), custom_call_target="tpu_custom_call", output_to_operand_aliasing={{0}: (5, {}), {1}: (6, {})} | custom-call | flops 3623878656 | bytes 14946816 | tf_op jit(solution)/shard_map/mlp2/pallas_call | solution.py:84
  167.8 10.6 %mlp0.1 = (f32[512,768]{1,0:T(8,128)}, f32[512,768]{1,0:T(8,128)}, f32[768,768]{1,0:T(8,128)}, f32[768,768]{1,0:T(8,128)}, f32[1,768]{1,0:T(1,128)S(1)}) custom-call(bf16[512,768]{1,0:T(8,128)(2,1)S(1)} %copy-done.50, bf16[512,768]{1,0:T(8,128)(2,1)S(1)} %copy-done.48, ...), custom_call_target="tpu_custom_call", output_to_operand_aliasing={{0}: (5, {}), {1}: (6, {})} | custom-call | flops 3623878656 | bytes 17306112 | tf_op jit(solution)/shard_map/mlp0/pallas_call | solution.py:84
  178.9 8.6 %post.1 = (bf16[512,768]{1,0:T(8,128)(2,1)}, f32[512,768]{1,0:T(8,128)S(1)}, bf16[512,192]{1,0:T(8,128)(2,1)S(1)}, bf16[512,192]{1,0:T(8,128)(2,1)S(1)}, bf16[51...) custom-call(f32[512,768]{1,0:T(8,128)} %get-tuple-element.109.bm, ...), custom_call_target="tpu_custom_call" | custom-call | flops 1207959552 | bytes 14595072 | tf_op jit(solution)/shard_map/post/pallas_call | solution.py:84
  187.6 2.7 convert.7
  203.3 7.0 %back3.1 = (bf16[512,192]{1,0:T(8,128)(2,1)S(1)}, f32[512,384]{1,0:T(8,128)S(1)}, f32[512,384]{1,0:T(8,128)S(1)}) custom-call(bf16[512,192]{1,0:T(8,128)(2,1)S(1)} %copy-done.88, bf16[1024,192]{1,0:T(8,128)(2,1)S(1)} %copy-done.78, bf16[1024,192]{1,0:T(8,128)(2,1)S(1)} %copy-done.80, bf16[512,192]{1,0:T(8,128)(2,1)S(1)} %copy-done.60, ...), custom_call_target="tpu_custom_call" | custom-call | flops 4026531840 | bytes 3227648 | tf_op jit(solution)/shard_map/back3/pallas_call | solution.py:84
  210.7 45.5 %collective-permute-done.43 = bf16[192,768]{1,0:T(8,128)(2,1)S(1)} collective-permute-done((bf16[192,768]{1,0:T(8,128)(2,1)S(1)}, bf16[192,768]{1,0:T(8,128)(2,1)S(1)}, u32[]{:S(2)}, u32[]{:S(2)}) %collective-permute-start.43) | collective-permute-done | bytes 294944 | tf_op jit(solution)/shard_map/ppermute | solution.py:383
  259.0 7.1 %back2.1 = (bf16[512,192]{1,0:T(8,128)(2,1)S(1)}, f32[512,384]{1,0:T(8,128)S(1)}, f32[512,384]{1,0:T(8,128)S(1)}) custom-call(bf16[512,192]{1,0:T(8,128)(2,1)S(1)} %copy-done.86, bf16[1024,192]{1,0:T(8,128)(2,1)S(1)} %copy-done.74, bf16[1024,192]{1,0:T(8,128)(2,1)S(1)} %copy-done.76, bf16[512,192]{1,0:T(8,128)(2,1)S(1)} %copy-done.58, ...), custom_call_target="tpu_custom_call" | custom-call | flops 4026531840 | bytes 3227648 | tf_op jit(solution)/shard_map/back2/pallas_call | solution.py:84
  268.0 7.3 %back0.1 = (bf16[512,192]{1,0:T(8,128)(2,1)S(1)}, f32[512,384]{1,0:T(8,128)S(1)}, f32[512,384]{1,0:T(8,128)S(1)}) custom-call(bf16[512,192]{1,0:T(8,128)(2,1)S(1)} %copy-done.84, bf16[1024,192]{1,0:T(8,128)(2,1)S(1)} %copy-done.70, bf16[1024,192]{1,0:T(8,128)(2,1)S(1)} %copy-done.72, bf16[512,192]{1,0:T(8,128)(2,1)S(1)} %copy-done.56, ...), custom_call_target="tpu_custom_call" | custom-call | flops 4026531840 | bytes 3227648 | tf_op jit(solution)/shard_map/back0/pallas_call | solution.py:84
  275.3 2.7 collective-permute-start.46
  278.0 7.1 %back1.1 = (bf16[512,192]{1,0:T(8,128)(2,1)S(1)}, f32[512,384]{1,0:T(8,128)S(1)}, f32[512,384]{1,0:T(8,128)S(1)}) custom-call(bf16[512,192]{1,0:T(8,128)(2,1)S(1)} %copy-done.82, bf16[1024,192]{1,0:T(8,128)(2,1)S(1)} %copy-done.66, bf16[1024,192]{1,0:T(8,128)(2,1)S(1)} %copy-done.68, bf16[512,192]{1,0:T(8,128)(2,1)S(1)} %copy-done.54, ...), custom_call_target="tpu_custom_call" | custom-call | flops 4026531840 | bytes 3227648 | tf_op jit(solution)/shard_map/back1/pallas_call | solution.py:84
  285.6 2.6 proj3.1
  288.2 2.5 collective-permute-done.47
  290.8 2.4 convert_add_fusion.1
  299.5 4.2 proj2.1
  307.0 3.6 collective-permute-done.51
  312.5 10.7 %collective-permute-done.58 = bf16[384,768]{1,0:T(8,128)(2,1)} collective-permute-done((bf16[384,768]{1,0:T(8,128)(2,1)}, bf16[384,768]{1,0:T(8,128)(2,1)}, u32[]{:S(2)}, u32[]{:S(2)}) %collective-permute-start.58) | collective-permute-done | bytes 589856 | tf_op jit(solution)/shard_map/ppermute | solution.py:383
  326.5 5.0 %collective-permute-done.52 = bf16[192,768]{1,0:T(8,128)(2,1)S(1)} collective-permute-done((bf16[192,768]{1,0:T(8,128)(2,1)S(1)}, bf16[192,768]{1,0:T(8,128)(2,1)S(1)}, u32[]{:S(2)}, u32[]{:S(2)}) %collective-permute-start.52) | collective-permute-done | bytes 294944 | tf_op jit(solution)/shard_map/ppermute | solution.py:383
  333.0 5.9 %collective-permute-done.59 = bf16[192,768]{1,0:T(8,128)(2,1)S(1)} collective-permute-done((bf16[192,768]{1,0:T(8,128)(2,1)S(1)}, bf16[192,768]{1,0:T(8,128)(2,1)S(1)}, u32[]{:S(2)}, u32[]{:S(2)}) %collective-permute-start.59) | collective-permute-done | bytes 294944 | tf_op jit(solution)/shard_map/ppermute | solution.py:383
  339.0 10.0 %collective-permute-done.53 = bf16[96,768]{1,0:T(8,128)(2,1)S(1)} collective-permute-done((bf16[96,768]{1,0:T(8,128)(2,1)S(1)}, bf16[96,768]{1,0:T(8,128)(2,1)S(1)}, u32[]{:S(2)}, u32[]{:S(2)}) %collective-permute-start.53) | collective-permute-done | bytes 147488 | tf_op jit(solution)/shard_map/ppermute | solution.py:383
  349.1 9.7 %collective-permute-done.60 = bf16[96,768]{1,0:T(8,128)(2,1)S(1)} collective-permute-done((bf16[96,768]{1,0:T(8,128)(2,1)S(1)}, bf16[96,768]{1,0:T(8,128)(2,1)S(1)}, u32[]{:S(2)}, u32[]{:S(2)}) %collective-permute-start.60) | collective-permute-done | bytes 147488 | tf_op jit(solution)/shard_map/ppermute | solution.py:383
  358.8 3.0 collective-permute-start.61
  362.7 3.5 collective-permute-done.54
  366.2 3.1 collective-permute-done.61
  372.1 2.9 proj0.1
  377.6 2.9 tail.1
  387.6 2.5 fusion.2
  394.9 4.4 collective-permute-done.28
  400.5 3.5 collective-permute-done.29
  408.5 4.2 collective-permute-done.36
  413.6 2.3 collective-permute-start.30
  415.8 7.3 %collective-permute-done.37 = bf16[72,768]{1,0:T(8,128)(2,1)S(1)} collective-permute-done((bf16[72,768]{1,0:T(8,128)(2,1)S(1)}, bf16[72,768]{1,0:T(8,128)(2,1)S(1)}, u32[]{:S(2)}, u32[]{:S(2)}) %collective-permute-start.37) | collective-permute-done | bytes 110624 | tf_op jit(solution)/shard_map/ppermute | solution.py:383
  423.3 7.6 %collective-permute-done.38 = bf16[72,768]{1,0:T(8,128)(2,1)S(1)} collective-permute-done((bf16[72,768]{1,0:T(8,128)(2,1)S(1)}, bf16[72,768]{1,0:T(8,128)(2,1)S(1)}, u32[]{:S(2)}, u32[]{:S(2)}) %collective-permute-start.38) | collective-permute-done | bytes 110624 | tf_op jit(solution)/shard_map/ppermute | solution.py:383
  431.9 3.5 fusion.5
  435.3 2.6 collective-permute-done.39
  439.2 2.9 fusion.1
  442.1 2.9 fusion
  445.0 3.8 collective-permute-done.40
  (423 shorter events, 113.2 us)
Async XLA Ops:
  0.6 11.7 %collective-permute-start.5 = (bf16[192,768]{1,0:T(8,128)(2,1)}, bf16[192,768]{1,0:T(8,128)(2,1)S(1)}, u32[]{:S(2)}, u32[]{:S(2)}) collective-permute-start(bf16[192,768]{1,0:T(8,128)(2,1)} %w0.3), channel_id=1, source_target_pairs={{0,2},{1,3},{2,0},{3,1},{4,6},{5,7},{6,4},{7,5},{8,10},{9,11},{10,... | collective-permute-start | bytes 884744 | tf_op jit(solution)/shard_map/ppermute | solution.py:383
  3.6 15.7 %collective-permute-start.4 = (bf16[192,768]{1,0:T(8,128)(2,1)}, bf16[192,768]{1,0:T(8,128)(2,1)S(1)}, u32[]{:S(2)}, u32[]{:S(2)}) collective-permute-start(bf16[192,768]{1,0:T(8,128)(2,1)} %w0.3), channel_id=1, source_target_pairs={{0,1},{1,0},{2,3},{3,2},{4,5},{5,4},{6,7},{7,6},{8,9},{9,8},{10,11... | collective-permute-start | bytes 884744 | tf_op jit(solution)/shard_map/ppermute | solution.py:383
  4.8 25.9 %collective-permute-start.2 = (bf16[576,768]{1,0:T(8,128)(2,1)}, bf16[576,768]{1,0:T(8,128)(2,1)}, u32[]{:S(2)}, u32[]{:S(2)}) collective-permute-start(bf16[576,768]{1,0:T(8,128)(2,1)} %bitcast.21), channel_id=1, source_target_pairs={{0,2},{1,3},{2,0},{3,1},{4,6},{5,7},{6,4},{7,5},{8,10},{9,11},{10,... | collective-permute-start | bytes 2654216 | tf_op jit(solution)/shard_map/ppermute | solution.py:383
  4.9 51.1 %collective-permute-start.7 = (bf16[768,768]{1,0:T(8,128)(2,1)}, bf16[768,768]{1,0:T(8,128)(2,1)}, u32[]{:S(2)}, u32[]{:S(2)}) collective-permute-start(bf16[768,768]{1,0:T(8,128)(2,1)} %wu.1), channel_id=1, source_target_pairs={{0,2},{1,3},{2,0},{3,1},{4,6},{5,7},{6,4},{7,5},{8,10},{9,11},{10,... | collective-permute-start | bytes 3538952 | tf_op jit(solution)/shard_map/ppermute | solution.py:383
  8.7 71.8 %collective-permute-start.9 = (bf16[768,768]{1,0:T(8,128)(2,1)}, bf16[768,768]{1,0:T(8,128)(2,1)}, u32[]{:S(2)}, u32[]{:S(2)}) collective-permute-start(bf16[768,768]{1,0:T(8,128)(2,1)} %wd.1), channel_id=1, source_target_pairs={{0,2},{1,3},{2,0},{3,1},{4,6},{5,7},{6,4},{7,5},{8,10},{9,11},{10,... | collective-permute-start | bytes 3538952 | tf_op jit(solution)/shard_map/ppermute | solution.py:383
  12.4 19.0 %collective-permute-start.1 = (bf16[576,768]{1,0:T(8,128)(2,1)}, bf16[576,768]{1,0:T(8,128)(2,1)S(1)}, u32[]{:S(2)}, u32[]{:S(2)}) collective-permute-start(bf16[576,768]{1,0:T(8,128)(2,1)} %bitcast.22), channel_id=1, source_target_pairs={{0,1},{1,0},{2,3},{3,2},{4,5},{5,4},{6,7},{7,6},{8,9},{9,8},{10,11... | collective-permute-start | bytes 2654216 | tf_op jit(solution)/shard_map/ppermute | solution.py:383
  19.4 11.4 %collective-permute-start = (bf16[512,768]{1,0:T(8,128)(2,1)S(1)}, bf16[512,768]{1,0:T(8,128)(2,1)S(1)}, u32[]{:S(2)}, u32[]{:S(2)}) collective-permute-start(bf16[512,768]{1,0:T(8,128)(2,1)S(1)} %get-tuple-element.91.h1o.h1), channel_id=1, source_target_pairs={{0,1},{1,0},{2,3},{3,2},{4,5},{5,4},{6,7},{7,6},{8,9},{9,8},{10,11... | collective-permute-start | bytes 2359304 | tf_op jit(solution)/shard_map/ppermute | solution.py:383
  30.8 68.3 %collective-permute-start.3 = (bf16[576,768]{1,0:T(8,128)(2,1)}, bf16[576,768]{1,0:T(8,128)(2,1)}, u32[]{:S(2)}, u32[]{:S(2)}) collective-permute-start(bf16[576,768]{1,0:T(8,128)(2,1)} %collective-permute-done.2.wt), channel_id=1, source_target_pairs={{0,1},{1,0},{2,3},{3,2},{4,5},{5,4},{6,7},{7,6},{8,9},{9,8},{10,11... | collective-permute-start | bytes 2654216 | tf_op jit(solution)/shard_map/ppermute | solution.py:383
  30.8 92.9 %collective-permute-start.13 = (bf16[768,768]{1,0:T(8,128)(2,1)}, bf16[768,768]{1,0:T(8,128)(2,1)S(1)}, u32[]{:S(2)}, u32[]{:S(2)}) collective-permute-start(bf16[768,768]{1,0:T(8,128)(2,1)} %wu.1), channel_id=1, source_target_pairs={{0,1},{1,0},{2,3},{3,2},{4,5},{5,4},{6,7},{7,6},{8,9},{9,8},{10,11... | collective-permute-start | bytes 3538952 | tf_op jit(solution)/shard_map/ppermute | solution.py:383
  31.4 92.3 %collective-permute-start.15 = (bf16[768,768]{1,0:T(8,128)(2,1)}, bf16[768,768]{1,0:T(8,128)(2,1)S(1)}, u32[]{:S(2)}, u32[]{:S(2)}) collective-permute-start(bf16[768,768]{1,0:T(8,128)(2,1)} %wd.1), channel_id=1, source_target_pairs={{0,1},{1,0},{2,3},{3,2},{4,5},{5,4},{6,7},{7,6},{8,9},{9,8},{10,11... | collective-permute-start | bytes 3538952 | tf_op jit(solution)/shard_map/ppermute | solution.py:383
  56.0 78.6 %collective-permute-start.10 = (bf16[768,768]{1,0:T(8,128)(2,1)}, bf16[768,768]{1,0:T(8,128)(2,1)S(1)}, u32[]{:S(2)}, u32[]{:S(2)}) collective-permute-start(bf16[768,768]{1,0:T(8,128)(2,1)} %collective-permute-done.7.wu), channel_id=1, source_target_pairs={{0,1},{1,0},{2,3},{3,2},{4,5},{5,4},{6,7},{7,6},{8,9},{9,8},{10,11... | collective-permute-start | bytes 3538952 | tf_op jit(solution)/shard_map/ppermute | solution.py:383
  80.5 54.2 %collective-permute-start.12 = (bf16[768,768]{1,0:T(8,128)(2,1)}, bf16[768,768]{1,0:T(8,128)(2,1)S(1)}, u32[]{:S(2)}, u32[]{:S(2)}) collective-permute-start(bf16[768,768]{1,0:T(8,128)(2,1)} %collective-permute-done.9.wd), channel_id=1, source_target_pairs={{0,1},{1,0},{2,3},{3,2},{4,5},{5,4},{6,7},{7,6},{8,9},{9,8},{10,11... | collective-permute-start | bytes 3538952 | tf_op jit(solution)/shard_map/ppermute | solution.py:383
  99.1 19.1 %collective-permute-start.6 = (bf16[192,768]{1,0:T(8,128)(2,1)S(1)}, bf16[192,768]{1,0:T(8,128)(2,1)S(1)}, u32[]{:S(2)}, u32[]{:S(2)}) collective-permute-start(bf16[192,768]{1,0:T(8,128)(2,1)S(1)} %collective-permute-done.5.w2), channel_id=1, source_target_pairs={{0,1},{1,0},{2,3},{3,2},{4,5},{5,4},{6,7},{7,6},{8,9},{9,8},{10,11... | collective-permute-start | bytes 884744 | tf_op jit(solution)/shard_map/ppermute | solution.py:383
  123.7 11.0 %collective-permute-start.11 = (bf16[1,768]{1,0:T(2,128)(2,1)S(1)}, bf16[1,768]{1,0:T(2,128)(2,1)S(1)}, u32[]{:S(2)}, u32[]{:S(2)}) collective-permute-start(bf16[1,768]{1,0:T(2,128)(2,1)S(1)} %collective-permute-done.8.bu), channel_id=1, source_target_pairs={{0,1},{1,0},{2,3},{3,2},{4,5},{5,4},{6,7},{7,6},{8,9},{9,8},{10,11... | collective-permute-start | bytes 4616 | tf_op jit(solution)/shard_map/ppermute | solution.py:383
  146.8 20.8 %collective-permute-start.18 = (bf16[768,768]{1,0:T(8,128)(2,1)}, bf16[768,768]{1,0:T(8,128)(2,1)}, u32[]{:S(2)}, u32[]{:S(2)}) collective-permute-start(bf16[768,768]{1,0:T(8,128)(2,1)} %get-tuple-element.107), channel_id=1, source_target_pairs={{0,1},{1,0},{2,3},{3,2},{4,5},{5,4},{6,7},{7,6},{8,9},{9,8},{10,11... | collective-permute-start | bytes 3538952 | tf_op jit(solution)/shard_map/ppermute | solution.py:383
  147.3 20.4 %collective-permute-start.19 = (bf16[768,768]{1,0:T(8,128)(2,1)}, bf16[768,768]{1,0:T(8,128)(2,1)}, u32[]{:S(2)}, u32[]{:S(2)}) collective-permute-start(bf16[768,768]{1,0:T(8,128)(2,1)} %get-tuple-element.108), channel_id=1, source_target_pairs={{0,1},{1,0},{2,3},{3,2},{4,5},{5,4},{6,7},{7,6},{8,9},{9,8},{10,11... | collective-permute-start | bytes 3538952 | tf_op jit(solution)/shard_map/ppermute | solution.py:383
  147.3 44.3 %collective-permute-start.31 = (bf16[2,128]{1,0:T(2,128)(2,1)}, bf16[2,128]{1,0:T(2,128)(2,1)}, u32[]{:S(2)}, u32[]{:S(2)}) collective-permute-start(bf16[2,128]{1,0:T(2,128)(2,1)} %param.18), channel_id=1, source_target_pairs={{0,4},{4,0},{8,12},{12,8},{16,20},{20,16},{24,28},{28,24},{1,5},{5... | collective-permute-start | bytes 1544 | tf_op jit(solution)/shard_map/ppermute | solution.py:383
  191.3 8.4 %collective-permute-start.42 = (bf16[192,768]{1,0:T(8,128)(2,1)}, bf16[192,768]{1,0:T(8,128)(2,1)}, u32[]{:S(2)}, u32[]{:S(2)}) collective-permute-start(bf16[192,768]{1,0:T(8,128)(2,1)} %get-tuple-element.174), channel_id=1, source_target_pairs={{0,1},{1,0},{2,3},{3,2},{4,5},{5,4},{6,7},{7,6},{8,9},{9,8},{10,11... | collective-permute-start | bytes 884744 | tf_op jit(solution)/shard_map/ppermute | solution.py:383
  197.5 93.2 %collective-permute-start.50 = (bf16[768,768]{1,0:T(8,128)(2,1)}, bf16[768,768]{1,0:T(8,128)(2,1)}, u32[]{:S(2)}, u32[]{:S(2)}) collective-permute-start(bf16[768,768]{1,0:T(8,128)(2,1)} %copy-done.44), channel_id=1, source_target_pairs={{0,2},{1,3},{2,0},{3,1},{4,6},{5,7},{6,4},{7,5},{8,10},{9,11},{10,... | collective-permute-start | bytes 3538952 | tf_op jit(solution)/shard_map/ppermute | solution.py:383
  197.8 96.4 %collective-permute-start.57 = (bf16[768,768]{1,0:T(8,128)(2,1)}, bf16[768,768]{1,0:T(8,128)(2,1)}, u32[]{:S(2)}, u32[]{:S(2)}) collective-permute-start(bf16[768,768]{1,0:T(8,128)(2,1)} %copy-done.43), channel_id=1, source_target_pairs={{0,2},{1,3},{2,0},{3,1},{4,6},{5,7},{6,4},{7,5},{8,10},{9,11},{10,... | collective-permute-start | bytes 3538952 | tf_op jit(solution)/shard_map/ppermute | solution.py:383
  199.6 11.1 %collective-permute-start.41 = (bf16[192,768]{1,0:T(8,128)(2,1)}, bf16[192,768]{1,0:T(8,128)(2,1)S(1)}, u32[]{:S(2)}, u32[]{:S(2)}) collective-permute-start(bf16[192,768]{1,0:T(8,128)(2,1)} %get-tuple-element.173), channel_id=1, source_target_pairs={{0,1},{1,0},{2,3},{3,2},{4,5},{5,4},{6,7},{7,6},{8,9},{9,8},{10,11... | collective-permute-start | bytes 884744 | tf_op jit(solution)/shard_map/ppermute | solution.py:383
  200.9 55.3 %collective-permute-start.43 = (bf16[192,768]{1,0:T(8,128)(2,1)S(1)}, bf16[192,768]{1,0:T(8,128)(2,1)S(1)}, u32[]{:S(2)}, u32[]{:S(2)}) collective-permute-start(bf16[192,768]{1,0:T(8,128)(2,1)S(1)} %add_convert_fusion), channel_id=1, source_target_pairs={{0,2},{1,3},{2,0},{3,1},{4,6},{5,7},{6,4},{7,5},{8,10},{9,11},{10,... | collective-permute-start | bytes 884744 | tf_op jit(solution)/shard_map/ppermute | solution.py:383
  210.4 88.4 %collective-permute-start.22 = (f32[512,384]{1,0:T(8,128)S(1)}, f32[512,384]{1,0:T(8,128)S(1)}, u32[]{:S(2)}, u32[]{:S(2)}) collective-permute-start(f32[512,384]{1,0:T(8,128)S(1)} %get-tuple-element.142), channel_id=1, source_target_pairs={{0,1},{1,0},{2,3},{3,2},{4,5},{5,4},{6,7},{7,6},{8,9},{9,8},{10,11... | collective-permute-start | bytes 2359304 | tf_op jit(solution)/shard_map/ppermute | solution.py:383
  257.4 8.8 %collective-permute-start.44 = (bf16[96,768]{1,0:T(8,128)(2,1)S(1)}, bf16[96,768]{1,0:T(8,128)(2,1)S(1)}, u32[]{:S(2)}, u32[]{:S(2)}) collective-permute-start(bf16[96,768]{1,0:T(8,128)(2,1)S(1)} %dynamic-slice_convert_fusion.8), channel_id=1, source_target_pairs={{0,4},{4,0},{8,12},{12,8},{16,20},{20,16},{24,28},{28,24},{1,5},{5... | collective-permute-start | bytes 442376 | tf_op jit(solution)/shard_map/ppermute | solution.py:383
  266.1 19.1 %collective-permute-start.23 = (f32[512,384]{1,0:T(8,128)S(1)}, f32[512,384]{1,0:T(8,128)S(1)}, u32[]{:S(2)}, u32[]{:S(2)}) collective-permute-start(f32[512,384]{1,0:T(8,128)S(1)} %get-tuple-element.145), channel_id=1, source_target_pairs={{0,1},{1,0},{2,3},{3,2},{4,5},{5,4},{6,7},{7,6},{8,9},{9,8},{10,11... | collective-permute-start | bytes 2359304 | tf_op jit(solution)/shard_map/ppermute | solution.py:383
  266.3 9.0 %collective-permute-start.45 = (bf16[48,768]{1,0:T(8,128)(2,1)S(1)}, bf16[48,768]{1,0:T(8,128)(2,1)S(1)}, u32[]{:S(2)}, u32[]{:S(2)}) collective-permute-start(bf16[48,768]{1,0:T(8,128)(2,1)S(1)} %dynamic-slice_convert_fusion.10), channel_id=1, source_target_pairs={{0,8},{4,12},{8,0},{12,4},{16,24},{20,28},{24,16},{28,20},{1,9},{5... | collective-permute-start | bytes 221192 | tf_op jit(solution)/shard_map/ppermute | solution.py:383
  275.3 9.8 %collective-permute-start.46 = (bf16[24,768]{1,0:T(8,128)(2,1)S(1)}, bf16[24,768]{1,0:T(8,128)(2,1)S(1)}, u32[]{:S(2)}, u32[]{:S(2)}) collective-permute-start(bf16[24,768]{1,0:T(8,128)(2,1)S(1)} %dynamic-slice_convert_fusion.11), channel_id=1, source_target_pairs={{0,16},{4,20},{8,24},{12,28},{16,0},{20,4},{24,8},{28,12},{1,17},{... | collective-permute-start | bytes 110600 | tf_op jit(solution)/shard_map/ppermute | solution.py:383
  285.1 18.6 %collective-permute-start.21 = (f32[512,384]{1,0:T(8,128)S(1)}, f32[512,384]{1,0:T(8,128)S(1)}, u32[]{:S(2)}, u32[]{:S(2)}) collective-permute-start(f32[512,384]{1,0:T(8,128)S(1)} %get-tuple-element.129), channel_id=1, source_target_pairs={{0,1},{1,0},{2,3},{3,2},{4,5},{5,4},{6,7},{7,6},{8,9},{9,8},{10,11... | collective-permute-start | bytes 2359304 | tf_op jit(solution)/shard_map/ppermute | solution.py:383
  294.2 16.4 %collective-permute-start.51 = (bf16[384,768]{1,0:T(8,128)(2,1)}, bf16[384,768]{1,0:T(8,128)(2,1)}, u32[]{:S(2)}, u32[]{:S(2)}) collective-permute-start(bf16[384,768]{1,0:T(8,128)(2,1)} %dynamic-slice_convert_fusion.1), channel_id=1, source_target_pairs={{0,4},{4,0},{8,12},{12,8},{16,20},{20,16},{24,28},{28,24},{1,5},{5... | collective-permute-start | bytes 1769480 | tf_op jit(solution)/shard_map/ppermute | solution.py:383
  297.3 26.0 %collective-permute-start.58 = (bf16[384,768]{1,0:T(8,128)(2,1)}, bf16[384,768]{1,0:T(8,128)(2,1)}, u32[]{:S(2)}, u32[]{:S(2)}) collective-permute-start(bf16[384,768]{1,0:T(8,128)(2,1)} %dynamic-slice_convert_fusion), channel_id=1, source_target_pairs={{0,4},{4,0},{8,12},{12,8},{16,20},{20,16},{24,28},{28,24},{1,5},{5... | collective-permute-start | bytes 1769480 | tf_op jit(solution)/shard_map/ppermute | solution.py:383
  298.8 72.3 %collective-permute-start.20 = (f32[512,384]{1,0:T(8,128)S(1)}, f32[512,384]{1,0:T(8,128)S(1)}, u32[]{:S(2)}, u32[]{:S(2)}) collective-permute-start(f32[512,384]{1,0:T(8,128)S(1)} %get-tuple-element.126), channel_id=1, source_target_pairs={{0,1},{1,0},{2,3},{3,2},{4,5},{5,4},{6,7},{7,6},{8,9},{9,8},{10,11... | collective-permute-start | bytes 2359304 | tf_op jit(solution)/shard_map/ppermute | solution.py:383
  298.9 59.9 %collective-permute-start.49 = (bf16[96,768]{1,0:T(8,128)(2,1)S(1)}, bf16[96,768]{1,0:T(8,128)(2,1)S(1)}, u32[]{:S(2)}, u32[]{:S(2)}) collective-permute-start(bf16[96,768]{1,0:T(8,128)(2,1)S(1)} %maximum_select_fusion.14), channel_id=1, source_target_pairs={{0,4},{4,0},{8,12},{12,8},{16,20},{20,16},{24,28},{28,24},{1,5},{5... | collective-permute-start | bytes 442376 | tf_op jit(solution)/shard_map/ppermute | solution.py:383
  306.8 65.3 %collective-permute-start.25 = (bf16[576,768]{1,0:T(8,128)(2,1)S(1)}, bf16[576,768]{1,0:T(8,128)(2,1)S(1)}, u32[]{:S(2)}, u32[]{:S(2)}) collective-permute-start(bf16[576,768]{1,0:T(8,128)(2,1)S(1)} %get-tuple-element.150), channel_id=1, source_target_pairs={{0,1},{1,0},{2,3},{3,2},{4,5},{5,4},{6,7},{7,6},{8,9},{9,8},{10,11... | collective-permute-start | bytes 2654216 | tf_op jit(solution)/shard_map/ppermute | solution.py:383
  310.6 70.0 %collective-permute-start.34 = (bf16[576,768]{1,0:T(8,128)(2,1)S(1)}, bf16[576,768]{1,0:T(8,128)(2,1)}, u32[]{:S(2)}, u32[]{:S(2)}) collective-permute-start(bf16[576,768]{1,0:T(8,128)(2,1)S(1)} %get-tuple-element.162), channel_id=1, source_target_pairs={{0,2},{1,3},{2,0},{3,1},{4,6},{5,7},{6,4},{7,5},{8,10},{9,11},{10,... | collective-permute-start | bytes 2654216 | tf_op jit(solution)/shard_map/ppermute | solution.py:383
  323.3 8.2 %collective-permute-start.52 = (bf16[192,768]{1,0:T(8,128)(2,1)S(1)}, bf16[192,768]{1,0:T(8,128)(2,1)S(1)}, u32[]{:S(2)}, u32[]{:S(2)}) collective-permute-start(bf16[192,768]{1,0:T(8,128)(2,1)S(1)} %dynamic-slice_convert_fusion.4), channel_id=1, source_target_pairs={{0,8},{4,12},{8,0},{12,4},{16,24},{20,28},{24,16},{28,20},{1,9},{5... | collective-permute-start | bytes 884744 | tf_op jit(solution)/shard_map/ppermute | solution.py:383
  338.9 10.1 %collective-permute-start.53 = (bf16[96,768]{1,0:T(8,128)(2,1)S(1)}, bf16[96,768]{1,0:T(8,128)(2,1)S(1)}, u32[]{:S(2)}, u32[]{:S(2)}) collective-permute-start(bf16[96,768]{1,0:T(8,128)(2,1)S(1)} %dynamic-slice_convert_fusion.7), channel_id=1, source_target_pairs={{0,16},{4,20},{8,24},{12,28},{16,0},{20,4},{24,8},{28,12},{1,17},{... | collective-permute-start | bytes 442376 | tf_op jit(solution)/shard_map/ppermute | solution.py:383
  349.0 9.8 %collective-permute-start.60 = (bf16[96,768]{1,0:T(8,128)(2,1)S(1)}, bf16[96,768]{1,0:T(8,128)(2,1)S(1)}, u32[]{:S(2)}, u32[]{:S(2)}) collective-permute-start(bf16[96,768]{1,0:T(8,128)(2,1)S(1)} %dynamic-slice_convert_fusion.6), channel_id=1, source_target_pairs={{0,16},{4,20},{8,24},{12,28},{16,0},{20,4},{24,8},{28,12},{1,17},{... | collective-permute-start | bytes 442376 | tf_op jit(solution)/shard_map/ppermute | solution.py:383
  358.8 10.5 %collective-permute-start.61 = (bf16[96,768]{1,0:T(8,128)(2,1)S(1)}, bf16[96,768]{1,0:T(8,128)(2,1)S(1)}, u32[]{:S(2)}, u32[]{:S(2)}) collective-permute-start(bf16[96,768]{1,0:T(8,128)(2,1)S(1)} %add_convert_fusion.1), channel_id=1, source_target_pairs={{0,16},{4,20},{8,24},{12,28},{16,0},{20,4},{24,8},{28,12},{1,17},{... | collective-permute-start | bytes 442376 | tf_op jit(solution)/shard_map/ppermute | solution.py:383
  366.2 65.7 %collective-permute-start.33 = (bf16[8,128]{1,0:T(8,128)(2,1)S(1)}, bf16[8,128]{1,0:T(8,128)(2,1)S(1)}, u32[]{:S(2)}, u32[]{:S(2)}) collective-permute-start(bf16[8,128]{1,0:T(8,128)(2,1)S(1)} %maximum_select_fusion.22), channel_id=1, source_target_pairs={{0,16},{4,20},{8,24},{12,28},{16,0},{20,4},{24,8},{28,12},{1,17},{... | collective-permute-start | bytes 6152 | tf_op jit(solution)/shard_map/ppermute | solution.py:383
  369.3 20.8 %collective-permute-start.55 = (bf16[192,768]{1,0:T(8,128)(2,1)S(1)}, bf16[192,768]{1,0:T(8,128)(2,1)}, u32[]{:S(2)}, u32[]{:S(2)}) collective-permute-start(bf16[192,768]{1,0:T(8,128)(2,1)S(1)} %maximum_select_fusion.8), channel_id=1, source_target_pairs={{0,8},{4,12},{8,0},{12,4},{16,24},{20,28},{24,16},{28,20},{1,9},{5... | collective-permute-start | bytes 884744 | tf_op jit(solution)/shard_map/ppermute | solution.py:383
  371.1 21.8 %collective-permute-start.62 = (bf16[192,768]{1,0:T(8,128)(2,1)}, bf16[192,768]{1,0:T(8,128)(2,1)}, u32[]{:S(2)}, u32[]{:S(2)}) collective-permute-start(bf16[192,768]{1,0:T(8,128)(2,1)} %maximum_select_fusion.9), channel_id=1, source_target_pairs={{0,8},{4,12},{8,0},{12,4},{16,24},{20,28},{24,16},{28,20},{1,9},{5... | collective-permute-start | bytes 884744 | tf_op jit(solution)/shard_map/ppermute | solution.py:383
  384.5 21.0 %collective-permute-start.35 = (bf16[288,768]{1,0:T(8,128)(2,1)}, bf16[288,768]{1,0:T(8,128)(2,1)}, u32[]{:S(2)}, u32[]{:S(2)}) collective-permute-start(bf16[288,768]{1,0:T(8,128)(2,1)} %dynamic-slice_convert_fusion.2), channel_id=1, source_target_pairs={{0,4},{4,0},{8,12},{12,8},{16,20},{20,16},{24,28},{28,24},{1,5},{5... | collective-permute-start | bytes 1327112 | tf_op jit(solution)/shard_map/ppermute | solution.py:383
  387.0 12.3 %collective-permute-start.28 = (f32[17,768]{1,0:T(8,128)S(1)}, f32[17,768]{1,0:T(8,128)S(1)}, u32[]{:S(2)}, u32[]{:S(2)}) collective-permute-start(f32[17,768]{1,0:T(8,128)S(1)} %pad_maximum_fusion.2), channel_id=1, source_target_pairs={{0,4},{4,0},{8,12},{12,8},{16,20},{20,16},{24,28},{28,24},{1,5},{5... | collective-permute-start | bytes 156680 | tf_op jit(solution)/shard_map/ppermute | solution.py:383
  391.4 50.7 %collective-permute-start.56 = (bf16[384,768]{1,0:T(8,128)(2,1)S(1)}, bf16[384,768]{1,0:T(8,128)(2,1)}, u32[]{:S(2)}, u32[]{:S(2)}) collective-permute-start(bf16[384,768]{1,0:T(8,128)(2,1)S(1)} %maximum_select_fusion.3), channel_id=1, source_target_pairs={{0,4},{4,0},{8,12},{12,8},{16,20},{20,16},{24,28},{28,24},{1,5},{5... | collective-permute-start | bytes 1769480 | tf_op jit(solution)/shard_map/ppermute | solution.py:383
  394.3 44.9 %collective-permute-start.63 = (bf16[384,768]{1,0:T(8,128)(2,1)S(1)}, bf16[384,768]{1,0:T(8,128)(2,1)}, u32[]{:S(2)}, u32[]{:S(2)}) collective-permute-start(bf16[384,768]{1,0:T(8,128)(2,1)S(1)} %maximum_select_fusion.4), channel_id=1, source_target_pairs={{0,4},{4,0},{8,12},{12,8},{16,20},{20,16},{24,28},{28,24},{1,5},{5... | collective-permute-start | bytes 1769480 | tf_op jit(solution)/shard_map/ppermute | solution.py:383
  412.8 10.4 %collective-permute-start.37 = (bf16[72,768]{1,0:T(8,128)(2,1)S(1)}, bf16[72,768]{1,0:T(8,128)(2,1)S(1)}, u32[]{:S(2)}, u32[]{:S(2)}) collective-permute-start(bf16[72,768]{1,0:T(8,128)(2,1)S(1)} %dynamic-slice_convert_fusion.9), channel_id=1, source_target_pairs={{0,16},{4,20},{8,24},{12,28},{16,0},{20,4},{24,8},{28,12},{1,17},{... | collective-permute-start | bytes 331784 | tf_op jit(solution)/shard_map/ppermute | solution.py:383
  413.6 17.5 %collective-permute-start.30 = (f32[53,768]{1,0:T(8,128)S(1)}, f32[53,768]{1,0:T(8,128)S(1)}, u32[]{:S(2)}, u32[]{:S(2)}) collective-permute-start(f32[53,768]{1,0:T(8,128)S(1)} %pad_maximum_fusion), channel_id=1, source_target_pairs={{0,16},{4,20},{8,24},{12,28},{16,0},{20,4},{24,8},{28,12},{1,17},{... | collective-permute-start | bytes 488456 | tf_op jit(solution)/shard_map/ppermute | solution.py:383
  438.0 10.7 %collective-permute-start.40 = (bf16[288,768]{1,0:T(8,128)(2,1)S(1)}, bf16[288,768]{1,0:T(8,128)(2,1)S(1)}, u32[]{:S(2)}, u32[]{:S(2)}) collective-permute-start(bf16[288,768]{1,0:T(8,128)(2,1)S(1)} %maximum_select_fusion.5), channel_id=1, source_target_pairs={{0,4},{4,0},{8,12},{12,8},{16,20},{20,16},{24,28},{28,24},{1,5},{5... | collective-permute-start | bytes 1327112 | tf_op jit(solution)/shard_map/ppermute | solution.py:383
  (127 other events, 1026.5 us)

commit v2 on v0

v2 whole, which is shorter than its diff:
```python
import functools

import jax
import jax.numpy as jnp
import numpy as np
from jax import lax
from jax.experimental import pallas as pl
from jax.experimental.pallas import tpu as pltpu
from jax.sharding import PartitionSpec as P

BF = jnp.bfloat16
F = jnp.float32
HD = 64
LEN = 1024
EPS = 1e-05
GELU_COEF = 0.7978845608028654
CUBIC_COEF = 0.044715
SCALE = 0.125
LOG2E = 1.4426950408889634
EXP_SCALE = SCALE * LOG2E
MIB = 1 << 20


def nn(a, b):
    return lax.dot_general(a, b, (((1,), (0,)), ((), ())), preferred_element_type=F)


def nt(a, b):
    return lax.dot_general(a, b, (((1,), (1,)), ((), ())), preferred_element_type=F)


def tn(a, b):
    return lax.dot_general(a, b, (((0,), (0,)), ((), ())), preferred_element_type=F)


def normalize(values):
    centered = values - jnp.mean(values, axis=-1, keepdims=True)
    inv = lax.rsqrt(jnp.mean(centered * centered, axis=-1, keepdims=True) + EPS)
    return centered * inv, inv


def layer_back(grad_norm, normed, inv):
    mean_grad = jnp.mean(grad_norm, axis=-1, keepdims=True)
    mean_cross = jnp.mean(grad_norm * normed, axis=-1, keepdims=True)
    return inv * (grad_norm - mean_grad - normed * mean_cross)


def halves_turned(v):
    parts = []
    for h in range(v.shape[1] // HD):
        lo = v[:, h * HD : h * HD + HD // 2]
        hi = v[:, h * HD + HD // 2 : (h + 1) * HD]
        parts += [-hi, lo]
    return jnp.concatenate(parts, axis=1)


def halves_back(v):
    parts = []
    for h in range(v.shape[1] // HD):
        lo = v[:, h * HD : h * HD + HD // 2]
        hi = v[:, h * HD + HD // 2 : (h + 1) * HD]
        parts += [hi, -lo]
    return jnp.concatenate(parts, axis=1)


def tables(block, heads):
    cos, sin = block[:, :HD], block[:, HD:]
    return jnp.concatenate([cos] * heads, axis=1), jnp.concatenate([sin] * heads, axis=1)


MESH = pl.DeviceIdType.MESH
PIECE = 256
HALVED = 3


def sds(shape, dtype):
    return jax.ShapeDtypeStruct(shape, dtype)


def split3(v):
    hi = v.astype(BF).astype(F)
    mid = (v - hi).astype(BF).astype(F)
    return hi, mid, v - hi - mid


def pick(index, values):
    out = jnp.int32(values[0])
    for i, v in enumerate(values[1:], 1):
        out = jnp.where(index == i, jnp.int32(v), out)
    return out


MLP_ORDER = [(1, 0), (1, 1), (1, 2), (3, 0), (2, 0), (0, 0), (0, 1), (3, 1), (2, 1), (0, 2), (3, 2), (2, 2)]
CROSS = [3, 6, 4, 7, 5, 8, 0, 1, 2]
SMALL_INPUTS = ("mask", "gain1", "gain2", "dbias", "upb", "adab", "time", "noise")


def block_kernel(n_dp, names, *args):
    ref = dict(zip(names, args))
    g = lambda *keys: [ref[key] for key in keys]
    tok_h, cot_h, prefix, ada_h, table_h, wt_h, wo_h, wu_h, wd_h = g("tok_h", "cot_h", "prefix", "ada_h", "table_h", "wt_h", "wo_h", "wu_h", "wd_h")
    out_o, gtok_o, grads_o, mods_o, small_o, wmu, wmd = g("out_o", "gtok_o", "grads_o", "mods_o", "small_o", "wmu", "wmd")
    w, wsu, wsd, rb, rx, sx, g0, sb, ry, rz1, rz2, exv = g("w", "wsu", "wsd", "rb", "rx", "sx", "g0", "sb", "ry", "rz1", "rz2", "exv")
    tok, cs, h1o, h1p, q, k, v, att, st, km = g("tok", "cs", "h1o", "h1p", "q", "k", "v", "att", "st", "km")
    branch, mixed, h2, gm, bm, gh, dk, dv, dq, parr, dwo2 = g(
        "branch", "mixed", "h2", "gm", "bm", "gh", "dk", "dv", "dq", "parr", "dwo2"
    )
    vecs, mod, nz, bus, gub, sums, mods, cse, cre, xse, xre, bse, bre = g(
        "vecs", "mod", "nz", "bus", "gub", "sums", "mods", "cse", "cre", "xse", "xre", "bse", "bre"
    )
    rows, d = tok.shape
    width = q.shape[2]
    heads = width // HD
    cond = ada_h.shape[0]
    tile = 256
    dp = lax.axis_index("dp")
    t = lax.axis_index("tensor")
    xb, cb = t // 2, t % 2
    bits = [1 << i for i in range(n_dp.bit_length() - 1)]
    bit = [(dp // b) % 2 for b in bits]
    core = (dp, t + 1 - 2 * cb)
    chip = (dp, t + 2 - 4 * xb)
    peer = [(dp + b - 2 * b * v_, t) for b, v_ in zip(bits, bit)]
    yb = bit[0]

    barrier = pltpu.get_barrier_semaphore()
    for other in [core, chip] + peer:
        pl.semaphore_signal(barrier, inc=1, device_id=other, device_id_type=MESH)
    pl.semaphore_wait(barrier, 2 + len(peer))

    def remote(src, dst, name, index, to):
        return pltpu.make_async_remote_copy(
            src_ref=src, dst_ref=dst, send_sem=ref[name + "_s"].at[index], recv_sem=ref[name + "_r"].at[index], device_id=to, device_id_type=MESH
        )

    def local(src, dst, index):
        return pltpu.make_async_copy(src, dst, ref["loc"].at[index])

    def at(start, size, mult=8):
        return pl.ds(start if isinstance(start, int) else pl.multiple_of(start, mult), size)

    att_src = [(wt_h, 0), (wt_h, width), (wt_h, 2 * width), (wo_h, 0)]
    hw = width // 2

    def part(r, j, which):
        if j < 4:
            return w.at[r, at(j * width + which * hw, hw, 32)]
        c, kind = (j - 4) // 2, (j - 4) % 2
        span = at(c * PIECE + which * 128, 128, 128)
        return wmd.at[r, span] if kind else wmu.at[r, :, span]

    def own_part(j, which):
        if j < 4:
            src, base = att_src[j]
            return src.at[at(base + which * hw, hw, 32)]
        c, kind = (j - 4) // 2, (j - 4) % 2
        span = at(c * PIECE + which * 128, 128, 128)
        return wd_h.at[span] if kind else wu_h.at[:, span]

    def far(j):
        return remote(own_part(j, yb), part(2, j, yb), "far", j, chip)

    def side(j):
        return remote(part(2, j, yb), part(2, j, yb), "side", j, peer[0])

    def cross(j, which):
        p = part(2, j, (yb + which) % 2)
        return remote(p, part(3, j, (yb + which) % 2), "cross", 2 * j + which, core)

    near = [
        remote(wt_h, w.at[1, pl.ds(0, 3 * width)], "near", 0, core),
        remote(wo_h, w.at[1, pl.ds(3 * width, width)], "near", 1, core),
        remote(wu_h, wmu.at[1], "near", 2, core),
        remote(wd_h, wmd.at[1], "near", 3, core),
    ]
    n_parts = 10

    def arrived(j):
        far(j).wait_recv()
        side(j).start()
        cross(j, 0).start()

    def passed(j):
        side(j).wait_recv()
        cross(j, 1).start()

    ada = sb
    loads = [local(ada_h.at[:, pl.ds(i * d, d)], ada.at[pl.ds(i * cond, cond)], i) for i in range(6)]
    load_tok, load_cot = local(tok_h, tok, 6), local(cot_h, h2, 7)
    load_cs = [local(table_h.at[at(cb * rows, rows)], cs.at[pl.ds(0, rows)], 8), local(table_h.at[at((1 - cb) * rows, rows)], cs.at[pl.ds(rows, rows)], 9)]
    load_w = [local(wt_h, w.at[0, pl.ds(0, 3 * width)], 10), local(wo_h, w.at[0, pl.ds(3 * width, width)], 11)]
    load_small = [local(ref[name], ref[name + "_v"], 52 + i) for i, name in enumerate(SMALL_INPUTS)]
    mask_v, gain1_v, gain2_v, dbias_v, upb_v, adab_v, time_v, noise_v = [ref[name + "_v"] for name in SMALL_INPUTS]
    for c in load_small + loads + [load_tok]:
        c.start()
    for c in load_small:
        c.wait()
    bus[0] = jnp.broadcast_to(upb_v[...].astype(F).reshape(1, -1), bus.shape[1:])
    bias_near, bias_far = remote(bus.at[0], bus.at[1], "bias", 0, core), remote(bus.at[0], bus.at[2], "bias", 1, chip)
    bias_cross = remote(bus.at[2], bus.at[3], "bias", 2, core)
    bias_near.start()
    bias_far.start()
    for j in range(n_parts):
        far(j).start()
    near[0].start()
    for c in load_w + load_cs + [load_cot]:
        c.start()

    for i, one in enumerate((mask_v, gain1_v, gain2_v, dbias_v)):
        vecs[i : i + 1, :] = one[...].astype(F).reshape(1, d)
    tv = jnp.where(xb == 0, time_v[0:1, :].astype(F), time_v[1:2, :].astype(F))
    s = jnp.broadcast_to(tv, (16, cond))
    s = s / (1.0 + jnp.exp(-s))
    stacked = jnp.concatenate(split3(s), axis=0).astype(BF)
    for i in range(6):
        loads[i].wait()
        m = nn(stacked, ada[pl.ds(i * cond, cond), :])
        mod[i : i + 1, :] = m[0:1] + m[16:17] + m[32:33] + adab_v[pl.ds(i * d, d)].astype(F).reshape(1, d)
    place = lax.broadcasted_iota(jnp.int32, (4, 128), 0) * 128 + lax.broadcasted_iota(jnp.int32, (4, 128), 1) + cb * rows
    limit = jnp.where(xb == 0, prefix[0], prefix[1])
    on = jnp.where((noise_v[...] == 1) & (place >= limit), 1.0, 0.0)
    on = jnp.concatenate([on, jnp.zeros((12, 128), F)], axis=0).astype(BF)
    eye = jnp.where(lax.broadcasted_iota(jnp.int32, (128, 128), 0) == lax.broadcasted_iota(jnp.int32, (128, 128), 1), 1.0, 0.0).astype(BF)
    cols = nt(eye, on)
    for i in range(4):
        nz[i * 128 : (i + 1) * 128, :] = cols[:, i : i + 1]
    load_tok.wait()

    def inputs_at(rs):
        return jnp.where(nz[rs, :] > 0.5, vecs[0:1, :], tok[rs, :].astype(F))

    every = pl.ds(0, rows)
    n1, _ = normalize(inputs_at(every))
    h1o[...] = (n1 * vecs[1:2, :] * (1.0 + mod[1:2, :]) + mod[0:1, :]).astype(BF)
    h1_copy = remote(h1o, h1p, "h1", 0, core)
    h1_copy.start()
    load_cot.wait()
    gmv = (mod[5:6, :] * h2[...].astype(F)).astype(BF)
    gm[...] = gmv
    sums[4:5, :] = jnp.sum(gmv.astype(F), axis=0, keepdims=True)
    for c in load_cs + load_w[:1]:
        c.wait()
    h1_copy.wait()
    for c in near[1:]:
        c.start()

    lane_q = lax.broadcasted_iota(jnp.int32, (rows, width), 1) // HD
    lane = lax.broadcasted_iota(jnp.int32, (tile, width), 1) // HD
    lane_s = lax.broadcasted_iota(jnp.int32, (tile, 128), 1)

    def project(r):
        cos, sin = tables(cs[0:rows, :], heads)
        qv = nt(h1o[...], w[r, 0:width, :])
        qv = (qv * cos + halves_turned(qv) * sin).astype(BF)
        q[r] = qv
        qf = qv.astype(F)
        for h in range(heads):
            km[h, 0:rows, :] = jnp.where(lane_q == h, qf, 0.0).astype(BF)
        kv = nt(h1o[...], w[r, width : 2 * width, :])
        k[r, 0:rows, :] = (kv * cos + halves_turned(kv) * sin).astype(BF)
        v[r, 0:rows, :] = nt(h1o[...], w[r, 2 * width : 3 * width, :]).astype(BF)
        cos, sin = tables(cs[rows : 2 * rows, :], heads)
        kv = nt(h1p[...], w[r, width : 2 * width, :])
        k[r, rows : 2 * rows, :] = (kv * cos + halves_turned(kv) * sin).astype(BF)
        v[r, rows : 2 * rows, :] = nt(h1p[...], w[r, 2 * width : 3 * width, :]).astype(BF)

    def attend(r, i):
        rs = at(i * tile, tile, tile)
        acc = jnp.zeros((tile, width), F)
        stats = jnp.zeros((tile, 128), F)
        for h in range(heads):
            s = nt(km[h, rs, :], k[r])
            m = jnp.max(s, axis=1, keepdims=True)
            e = jnp.exp2((s - m) * EXP_SCALE)
            total = jnp.sum(e, axis=1, keepdims=True)
            p = (e * (1.0 / total)).astype(BF)
            acc = jnp.where(lane == h, nn(p, v[r]), acc)
            stats = jnp.where(lane_s == h, m * EXP_SCALE + jnp.log2(total), stats)
        att[r, rs, :] = acc.astype(BF)
        dq[rs, 0:128] = stats

    def at_step(step, todo):
        for key, fns in todo.items():

            @pl.when(step == key)
            def _():
                for fn in fns:
                    fn()

    def wait_near(i):
        return near[i].wait_recv

    def wait_cross(j):
        def go():
            cross(j, 0).wait_recv()
            cross(j, 1).wait_recv()

        return go

    arrive = lambda j: functools.partial(arrived, j)
    go_on = lambda j: functools.partial(passed, j)
    per_r = rows // tile

    def bias_on():
        bias_far.wait_recv()
        bias_cross.start()

    fwd_plan = {
        0: [arrive(0)],
        1: [arrive(1), bias_on],
        2: [wait_near(0), arrive(2), go_on(0)],
        3: [arrive(3), go_on(1)],
        4: [go_on(2)],
        5: [arrive(4), go_on(3)],
        6: [wait_cross(0), wait_cross(1), wait_cross(2)],
        7: [arrive(5), go_on(4)],
    }

    def fwd_body(it, carry):
        r, i = it // per_r, it % per_r
        at_step(it, fwd_plan)

        @pl.when(i == 0)
        def _():
            project(r)

        attend(r, i)

        @pl.when(i == per_r - 1)
        def _():
            st[r] = dq[:, 0:128].T[0:8, :]

        return carry

    lax.fori_loop(0, 4 * per_r, fwd_body, 0)
    arrived(6)
    load_w[1].wait()
    wait_near(1)()
    wait_cross(3)()

    def mid_body(i, carry):
        rs = at(i * tile, tile, tile)
        b = nn(att[0, rs, :], w[0, 3 * width : 4 * width, :])
        for r in range(1, 4):
            b = b + nn(att[r, rs, :], w[r, 3 * width : 4 * width, :])
        x = inputs_at(rs) + mod[2:3, :] * b
        n2, _ = normalize(x)
        branch[rs, :] = b
        mixed[rs, :] = x
        h2[rs, :] = (n2 * vecs[2:3, :] * (1.0 + mod[4:5, :]) + mod[3:4, :]).astype(BF)
        bm[rs, :] = jnp.zeros((tile, d), F)
        gh[rs, :] = jnp.zeros((tile, d), F)
        return carry

    lax.fori_loop(0, per_r, mid_body, 0)
    load_cot = local(cot_h, tok, 7)
    load_cot.start()

    def piece(buf, p, start=0, size=PIECE):
        return buf.at[at(p * PIECE + start, size)]

    def cross_send(n):
        p = CROSS[n]
        return remote(piece(sx, p), piece(rx, p), "gx", p, chip)

    off1 = yb * 128
    off2 = off1 + bit[1] * 64
    off3 = off2 + bit[2] * 32
    anti1 = (1 - yb) * 128
    anti2 = off1 + (1 - bit[1]) * 64
    anti3 = off2 + (1 - bit[2]) * 32

    def sl(p, start, size):
        return at(p * PIECE + start, size, 32)

    def send_y(p):
        return remote(rx.at[pl.ds(p * PIECE, 128)], ry.at[p], "gy", p, peer[0])

    def send_z1(p):
        return remote(rx.at[pl.ds(p * PIECE + 128, 64)], rz1.at[p], "gz", p, peer[1])

    def send_z2(p):
        return remote(rx.at[pl.ds(p * PIECE + 192, 32)], rz2.at[p], "gw", p, peer[2])

    def back_z2(p):
        return remote(sx.at[sl(p, off3, 32)], sx.at[sl(p, off3, 32)], "aw", p, peer[2])

    def back_z1(p):
        return remote(sx.at[sl(p, off2, 64)], sx.at[sl(p, off2, 64)], "az", p, peer[1])

    def back_y(p):
        return remote(sx.at[sl(p, off1, 128)], sx.at[sl(p, off1, 128)], "ay", p, peer[0])

    def more(e, p):
        return remote(g0.at[sl(p, off3, 32)], ref["ex"].at[e, p], "ge", e * 9 + p, peer[HALVED + e])

    def stage_x(n):
        p = CROSS[n]
        cross_send(n).wait()
        g0[piece_ds(p), :] = g0[piece_ds(p), :] + rx[piece_ds(p), :].astype(F)
        rx[pl.ds(p * PIECE, 128), :] = g0[sl(p, anti1, 128), :].astype(BF)
        send_y(p).start()

    def piece_ds(p):
        return pl.ds(p * PIECE, PIECE)

    def stage_y(n):
        p = CROSS[n]
        send_y(p).wait_recv()
        g0[sl(p, off1, 128), :] = g0[sl(p, off1, 128), :] + ry[p].astype(F)
        rx[pl.ds(p * PIECE + 128, 64), :] = g0[sl(p, anti2, 64), :].astype(BF)
        send_z1(p).start()

    def stage_z1(n):
        p = CROSS[n]
        send_z1(p).wait_recv()
        g0[sl(p, off2, 64), :] = g0[sl(p, off2, 64), :] + rz1[p].astype(F)
        rx[pl.ds(p * PIECE + 192, 32), :] = g0[sl(p, anti3, 32), :].astype(BF)
        send_z2(p).start()

    def stage_z2(n):
        p = CROSS[n]
        send_z2(p).wait_recv()
        total = g0[sl(p, off3, 32), :] + rz2[p].astype(F)
        for e in range(len(bits) - HALVED):
            g0[sl(p, off3, 32), :] = total
            more(e, p).start()
            more(e, p).wait()
            fill = local(ref["ex"].at[e, p], exv, 36)
            fill.start()
            fill.wait()
            total = total + exv[...]
        sx[sl(p, off3, 32), :] = total.astype(BF)
        back_z2(p).start()

    def stage_a1(n):
        p = CROSS[n]
        back_z2(p).wait_recv()
        back_z1(p).start()

    def stage_a2(n):
        p = CROSS[n]
        back_z1(p).wait_recv()
        back_y(p).start()

    def result(p):
        return local(sx.at[piece_ds(p)], grads_o.at[piece_ds(p)], 14 + p)

    def stage_a3(n):
        p = CROSS[n]
        back_y(p).wait_recv()
        result(p).start()

    def stage_end(n):
        p = CROSS[n]
        send_y(p).wait_send()
        send_z1(p).wait_send()
        send_z2(p).wait_send()
        back_z2(p).wait_send()
        back_z1(p).wait_send()
        back_y(p).wait_send()
        result(p).wait()

    stages = dict(X=stage_x, Y=stage_y, Z=stage_z1, W=stage_z2, A=stage_a1, B=stage_a2, C=stage_a3, E=stage_end)

    def run(text):
        for i in range(0, len(text), 2):
            stages[text[i]](int(text[i + 1]))

    steps = len(MLP_ORDER)

    def core_slot(step):
        return 2 * (sum(1 for r, _ in MLP_ORDER[:step] if r % 2) % 3)

    def give(step, kind):
        r, c = MLP_ORDER[step]
        slot = core_slot(step) + kind
        row = (3 * kind + c) * PIECE
        return remote(sb.at[pl.ds(slot * PIECE, PIECE)], rb.at[r // 2, pl.ds(row, PIECE)], "give", 2 * step + kind, core)

    def fetch(step, slot, own):
        r = pick(step, [r for r, _ in MLP_ORDER])
        c = pick(step, [c for _, c in MLP_ORDER])
        span = at(c * PIECE, PIECE, PIECE)
        up, down = (wu_h, wd_h) if own else (wmu.at[r], wmd.at[r])
        return [
            pltpu.make_async_copy(up.at[:, span], wsu.at[slot], ref["wst"].at[slot, 0]),
            pltpu.make_async_copy(down.at[span], wsd.at[slot], ref["wst"].at[slot, 1]),
        ]

    bias_near.wait_recv()
    for i in (2, 3):
        near[i].wait_recv()
    for c in fetch(0, 0, False):
        c.start()

    mlp_plan = {
        1: [go_on(5), arrive(7)],
        2: [wait_cross(4), wait_cross(5), go_on(6)],
        4: [arrive(8), go_on(7)],
        6: [wait_cross(6), wait_cross(7), arrive(9)],
        8: [go_on(8)],
        9: [go_on(9), wait_cross(8), wait_cross(9)],
    }

    def mlp_body(step, carry):
        slot = step % 2
        r = pick(step, [r for r, _ in MLP_ORDER])
        c = pick(step, [c for _, c in MLP_ORDER])
        at_step(step, mlp_plan)
        for cp in fetch(step, slot, False):
            cp.wait()

        nxt = pick(step, [r for r, _ in MLP_ORDER[1:]] + [4])

        @pl.when((nxt > 0) & (nxt < 4))
        def _():
            for cp in fetch(step + 1, 1 - slot, False):
                cp.start()

        @pl.when(nxt == 0)
        def _():
            for cp in fetch(step + 1, 1 - slot, True):
                cp.start()

        @pl.when(step == 0)
        def _():
            bias_cross.wait_recv()

        cols = at(c * PIECE, PIECE, PIECE)
        u = nn(h2[...], wsu[slot]) + bus[r, 0:1, cols]
        th = jnp.tanh(GELU_COEF * (u + CUBIC_COEF * u * u * u))
        act = (0.5 * u * (1.0 + th)).astype(BF)
        slope = 0.5 * (1.0 + th) + 0.5 * u * (1.0 - th * th) * GELU_COEF * (1.0 + 3.0 * CUBIC_COEF * u * u)
        gu_f = (nt(gm[...], wsd[slot]) * slope).astype(BF).astype(F)
        gu = gu_f.astype(BF)
        gub[r, 0:1, cols] = jnp.sum(gu_f, axis=0, keepdims=True)
        bm[...] += nn(act, wsd[slot])
        gh[...] += nt(gu, wsu[slot])
        ds_ = (tn(gu, h2[...]), tn(act, gm[...]))
        for i, (r_, c_) in enumerate(MLP_ORDER):

            @pl.when(step == i)
            def _():
                rows_ = [pl.ds((3 + 3 * kind + c_) * PIECE, PIECE) for kind in range(2)]
                inbox = [pl.ds((3 * kind + c_) * PIECE, PIECE) for kind in range(2)]
                if r_ % 2:
                    before = [j for j in range(i) if MLP_ORDER[j][0] % 2 and core_slot(j) == core_slot(i)]
                    for kind in range(2):
                        if before:
                            give(before[-1], kind).wait_send()
                        sb[pl.ds((core_slot(i) + kind) * PIECE, PIECE), :] = ds_[kind].astype(BF)
                        give(i, kind).start()
                else:
                    origin = MLP_ORDER.index((r_ + 1, c_))
                    for kind in range(2):
                        give(origin, kind).wait_recv()
                        total = ds_[kind] + rb[r_ // 2, inbox[kind], :].astype(F)
                        if r_ == 2:
                            sx[rows_[kind], :] = total.astype(BF)
                            cross_send(CROSS.index(3 + 3 * kind + c_)).start()
                        else:
                            g0[rows_[kind], :] = total

        return carry

    lax.fori_loop(0, steps, mlp_body, 0)
    odd = [i for i, (r, _) in enumerate(MLP_ORDER) if r % 2]
    for i in odd[-3:]:
        for kind in range(2):
            give(i, kind).wait_send()

    load_cot.wait()
    run("X0")
    gba = h1p

    def post_body(i, carry):
        rs = at(i * tile, tile, tile)
        x = mixed[rs, :]
        n2, inv = normalize(x)
        c = tok[rs, :].astype(F)
        bmlp = bm[rs, :] + vecs[3:4, :]
        h2[rs, :] = (x + mod[5:6, :] * bmlp).astype(BF)
        gr = gh[rs, :]
        gs = gr * (1.0 + mod[4:5, :])
        gmix = c + layer_back(gs * vecs[2:3, :], n2, inv)
        mixed[rs, :] = gmix
        gba[rs, :] = (mod[2:3, :] * gmix).astype(BF)
        part_sums = [gs * n2, gmix * branch[rs, :], gr, gr * n2 * vecs[2:3, :], c * bmlp]
        for row, val in zip((3, 10, 11, 12, 13), part_sums):
            got = jnp.sum(val, axis=0, keepdims=True)

            @pl.when(i == 0)
            def _():
                sums[row : row + 1, :] = got

            @pl.when(i > 0)
            def _():
                sums[row : row + 1, :] += got

        return carry

    lax.fori_loop(0, per_r, post_body, 0)
    store_out = local(h2, out_o, 26)
    store_out.start()
    load_tok = local(tok_h, tok, 6)
    load_tok.start()
    run("")
    for r in range(4):
        wo = w[r, 3 * width : 4 * width, :]
        dw = tn(att[r], gba[...])
        att[r] = nt(gba[...], wo).astype(BF)
        if r == 0:
            g0[pl.ds(3 * width, width), :] = dw
        elif r == 2:
            dwo2[...] = dw
        else:
            sb[pl.ds((3 - r) // 2 * 4 * width + 3 * width, width), :] = dw.astype(BF)

    lane_k = lax.broadcasted_iota(jnp.int32, (2 * rows, width), 1) // HD

    def back_tile(r, i, it):
        @pl.when(i == 0)
        def _():
            kf = k[r].astype(F)
            for h in range(heads):
                km[h] = jnp.where(lane_k == h, kf, 0.0).astype(BF)
            dk[...] = jnp.zeros_like(dk)
            dv[...] = jnp.zeros_like(dv)

        rs = at(i * tile, tile, tile)
        qt = q[r, rs, :].astype(F)
        gt = att[r, rs, :].astype(F)
        acc = jnp.zeros((tile, width), F)
        for h in range(heads):
            back_events(it, h)
            qm = jnp.where(lane == h, qt, 0.0).astype(BF)
            gmh = jnp.where(lane == h, gt, 0.0).astype(BF)
            p = jnp.exp2(nt(k[r], qm) * EXP_SCALE - st[r, h : h + 1, rs])
            dpr = nt(v[r], gmh)
            inner = jnp.sum(p * dpr, axis=0, keepdims=True)
            ds_ = (p * (dpr - inner)).astype(BF)
            dv[...] += nn(p.astype(BF), gmh)
            dk[...] += nn(ds_, qm)
            acc = acc + tn(ds_, km[h])
        dq[rs, :] = acc

    def par_copy(r):
        lanes = pl.ds((r % 2) * 2 * width, 2 * width)
        return remote(branch.at[:, lanes], parr.at[r % 2], "par", r, core)

    def finish_back(r):
        cos, sin = tables(cs[0:rows, :], heads)
        gq = dq[...] * SCALE
        q[r] = (gq * cos + halves_back(gq * sin)).astype(BF)
        lanes = slice((r % 2) * 2 * width, (r % 2) * 2 * width + 2 * width)
        bm[:, lanes] = jnp.concatenate([dk[0:rows, :] * SCALE, dv[0:rows, :]], axis=1)
        if r < 2:
            par_copy(r + 2).wait_send()
            if r == 1:
                pl.semaphore_wait(ref["credit"], 1)
        branch[:, lanes] = jnp.concatenate([dk[rows : 2 * rows, :] * SCALE, dv[rows : 2 * rows, :]], axis=1)
        par_copy(r).start()

    def hand(r):
        base = (3 - r) // 2 * 4 * width
        return remote(sb.at[pl.ds(base, 4 * width)], rb.at[r // 2, pl.ds(0, 4 * width)], "hand", r // 2, core)

    def weight_grads(r):
        par_copy(r ^ 1).wait_recv()
        cos, sin = tables(cs[0:rows, :], heads)
        lanes = slice((r % 2) * 2 * width, (r % 2) * 2 * width + 2 * width)
        gkv = bm[:, lanes] + parr[(r ^ 1) % 2]
        gk = gkv[:, :width]
        gk = (gk * cos + halves_back(gk * sin)).astype(BF)
        gv = gkv[:, width:].astype(BF)
        parts = (q[r], gk, gv)
        if r % 2 == 0:
            hand(r + 1).wait_recv()
        back = 0.0 if r == 3 else gh[...]
        for i, p_ in enumerate(parts):
            place_ = pl.ds(i * width, width)
            back = back + nn(p_, w[r, i * width : (i + 1) * width, :])
            dw = tn(p_, h1o[...])
            if r % 2:
                sb[pl.ds((3 - r) // 2 * 4 * width + i * width, width), :] = dw.astype(BF)
            else:
                dw = dw + rb[r // 2, place_, :].astype(F)
                if r == 2:
                    sx[place_, :] = dw.astype(BF)
                else:
                    g0[place_, :] = dw
        gh[...] = back
        place_ = pl.ds(3 * width, width)
        if r % 2:
            hand(r).start()
        elif r == 2:
            sx[place_, :] = (dwo2[...] + rb[1, place_, :].astype(F)).astype(BF)
            for n in (6, 7, 8):
                cross_send(n).start()
        else:
            g0[place_, :] = g0[place_, :] + rb[0, place_, :].astype(F)

    def give_credit():
        pl.semaphore_signal(ref["credit"], inc=1, device_id=core, device_id_type=MESH)

    back_plan = [
        {0: "X1Y0", 2: "X2", 4: "W1X3", 5: "Z2A1Y3X4", 6: "W2"},
        {1: "Z0", 2: "W0", 3: "A0", 4: "B0", 5: "C0", 6: "B1", 7: "A2"},
        {1: "Y1", 2: "Z1", 3: "Y2", 6: "Y4X5Z3", 7: "C1Z4"},
    ]

    def back_events(it, h):
        at_step(it, {key: [functools.partial(run, text)] for key, text in back_plan[h].items()})

    def back_body(it, carry):
        i = it % per_r
        back_tile(3 - it // per_r, i, it)
        for r in range(4):

            @pl.when(it == (3 - r) * per_r + per_r - 1)
            def _():
                finish_back(r)

        @pl.when(it == 2 * per_r)
        def _():
            weight_grads(3)
            weight_grads(2)
            give_credit()

        return carry

    lax.fori_loop(0, 4 * per_r, back_body, 0)
    run("")
    weight_grads(1)
    run("W3Y5B2")
    weight_grads(0)

    hand(1).wait_send()
    hand(3).wait_send()
    store_out.wait()
    load_tok.wait()
    run("X6W4")

    def tail_body(i, carry):
        rs = at(i * tile, tile, tile)
        on_ = nz[rs, :] > 0.5
        n1_, inv = normalize(inputs_at(rs))
        gr = gh[rs, :]
        gs = gr * (1.0 + mod[1:2, :])
        gi = mixed[rs, :] + layer_back(gs * vecs[1:2, :], n1_, inv)
        mixed[rs, :] = jnp.where(on_, 0.0, gi)
        part_sums = [gs * n1_, jnp.where(on_, gi, 0.0), gr, gr * n1_ * vecs[1:2, :]]
        for row, val in zip((1, 2, 8, 9), part_sums):
            got = jnp.sum(val, axis=0, keepdims=True)

            @pl.when(i == 0)
            def _():
                sums[row : row + 1, :] = got

            @pl.when(i > 0)
            def _():
                sums[row : row + 1, :] += got

        return carry

    lax.fori_loop(0, per_r, tail_body, 0)
    store_tok = local(mixed, gtok_o, 27)
    store_tok.start()
    run("A3C2Z5")

    none = jnp.zeros((2, d), F)
    cse[0:8, :] = jnp.concatenate([sums[8:14, :], none], axis=0)
    cse[8:16, :] = jnp.concatenate([gub[1, 0:1, :], gub[3, 0:1, :], sums[1:5, :], none], axis=0)
    core_sum = remote(cse, cre, "sc", 0, core)
    core_sum.start()
    run("")
    core_sum.wait_recv()
    own_mods = cse[0:6, :] + cre[0:6, :]
    tv_row = jnp.concatenate([tv, jnp.zeros((1, d - cond), F)], axis=1)
    me = 2 * dp + xb
    mods[me] = jnp.concatenate([own_mods, tv_row, jnp.zeros((1, d), F)], axis=0)
    xse[...] = jnp.concatenate([gub[2, 0:1, :] + cre[9:10, :], cse[10:14, :] + cre[10:14, :], jnp.zeros((3, d), F)], axis=0)
    chip_sum = remote(xse, xre, "sx", 0, chip)
    chip_mods = remote(mods.at[me], mods.at[me], "sx", 1, chip)
    chip_sum.start()
    chip_mods.start()
    run("X7A4Y6B3")
    chip_sum.wait_recv()
    cur = jnp.concatenate([gub[0, 0:1, :] + cre[8:9, :] + xre[0:1, :], xse[1:8, :] + xre[1:8, :]], axis=0)
    chip_mods.wait()
    pending = [core_sum, chip_sum]
    drain = ["W5", "B4", "Y7X8Z6"]
    for i, b in enumerate(bits):
        bse[i] = cur
        base = (dp // b) * b * 2
        one = remote(bse.at[i], bre.at[i], "sd", 2 * i, peer[i])
        two = remote(mods.at[pl.ds(base, 2 * b)], mods.at[pl.ds(base, 2 * b)], "sd", 2 * i + 1, peer[i])
        one.start()
        two.start()
        if drain:
            run(drain.pop(0))
        one.wait_recv()
        two.wait()
        pending.append(one)
        cur = cur + bre[i]
    small_o[...] = cur
    for text in drain:
        run(text)
    store_mods = local(mods, mods_o, 28)
    store_mods.start()
    run("A5C3Z7W6")
    run("C4B5W7Y8")
    run("A6A7C5Z8")
    run("B6B7W8C6")
    run("A8C7B8C8")
    for n in range(9):
        stage_end(n)
    for c in [store_mods, store_tok]:
        c.wait()
    for c in pending:
        c.wait_send()
    for c in near + [bias_near, bias_far, bias_cross]:
        c.wait_send()
    for j in range(n_parts):
        far(j).wait_send()
        side(j).wait_send()
        cross(j, 0).wait_send()
        cross(j, 1).wait_send()
    for r in range(2):
        par_copy(r).wait_send()


def finish_kernel(n_dp, grads_h, out_h, tok_h, mods_h, small, ada_h, time, out_o, gtok_o, gqkv_o, gout_o, gup_o, gdown_o, gada_o, gtime_o, gadab_o, gmask_o, ga_o, gm_o, gub_o, gdb_o, grads, wide, outv, tokv, mods, ada, adag, sem):
    d = grads.shape[1]
    width = gout_o.shape[0]
    cond = ada.shape[0]
    seqs = mods.shape[0]
    dp = lax.axis_index("dp")

    def copy(src, dst, index):
        return pltpu.make_async_copy(src, dst, sem.at[index])

    span = lambda p: pl.ds(p * PIECE, PIECE)
    load_mods, load_ada = copy(mods_h, mods, 0), copy(ada_h, ada, 1)
    load_tok, load_out = copy(tok_h, tokv, 2), copy(out_h, outv, 3)
    pieces = [copy(grads_h.at[span(p)], grads.at[span(p)], 4 + p) for p in range(9)]
    for c in [load_mods] + pieces + [load_tok, load_out, load_ada]:
        c.start()
    stores = []

    def store(src, dst):
        stores.append(copy(src, dst, 13 + len(stores)))
        stores[-1].start()

    head = 3 * width
    for p in range(9):
        pieces[p].wait()
        if 3 <= p < 6:
            for b in range(3):
                wide[span(p), span(b)] = grads[span(p), span(b)].astype(F).T
                store(wide.at[span(p), span(b)], gup_o.at[span(b), span(p - 3)])
        else:
            wide[span(p), :] = grads[span(p), :].astype(F)
            if p >= 6:
                store(wide.at[span(p)], gdown_o.at[span(p - 6)])
            elif p == 2:
                store(wide.at[pl.ds(0, head)], gqkv_o)
                store(wide.at[pl.ds(head, width)], gout_o)
    load_tok.wait()
    store(tokv, gtok_o)
    load_out.wait()
    store(outv, out_o)
    load_mods.wait()
    total = mods[0]
    for s_ in range(1, seqs):
        total = total + mods[s_]
    tall = jnp.concatenate([mods[s_, 6:7, 0:cond] for s_ in range(seqs)], axis=0)
    left = split3(tall / (1.0 + jnp.exp(-tall)))
    lhs = jnp.concatenate([left[0], left[0], left[1], left[0], left[2], left[1]], axis=0).astype(BF)
    for j in range(6):
        gadab_o[pl.ds(j * d, d)] = total[j : j + 1, :].reshape(d)
        right = split3(jnp.concatenate([mods[s_, j : j + 1, :] for s_ in range(seqs)], axis=0))
        rhs = jnp.concatenate([right[0], right[1], right[0], right[2], right[0], right[1]], axis=0).astype(BF)
        adag[j] = tn(lhs, rhs)
        store(adag.at[j], gada_o.at[:, pl.ds(j * d, d)])
    load_ada.wait()
    acc = jnp.zeros((48, cond), F)
    for j in range(6):
        pairs = jnp.concatenate([mods[2 * dp, j : j + 1, :], mods[2 * dp + 1, j : j + 1, :], jnp.zeros((14, d), F)], axis=0)
        acc = acc + nt(jnp.concatenate(split3(pairs), axis=0).astype(BF), ada[:, pl.ds(j * d, d)])
    te = time[...].astype(F)
    sig = 1.0 / (1.0 + jnp.exp(-te))
    gtime_o[...] = (acc[0:2] + acc[16:18] + acc[32:34]) * sig * (1.0 + te * (1.0 - sig))
    for row, o in enumerate((gub_o, ga_o, gmask_o, gm_o, gdb_o)):
        o[...] = small[row : row + 1, :].reshape(d)
    for c in stores:
        c.wait()


def rotary_block():
    freq = np.float32(10000.0) ** (np.float32(-2.0) * np.arange(HD // 2, dtype=np.float32) / np.float32(HD))
    angle = np.arange(LEN, dtype=np.float32)[:, None] * freq[None, :].astype(np.float32)
    angle = np.concatenate([angle, angle], axis=1)
    return np.concatenate([np.cos(angle), np.sin(angle)], axis=1).astype(np.float32)


def per_device(tokens, time_emb, prefix_len, noise_mask, mask_embed, gain_attn, gain_mlp, ada_weight, ada_bias, qkv_weight, out_weight, up_weight, up_bias, down_weight, down_bias, cotangent):
    rows, d = tokens.shape
    n_dp = lax.axis_size("dp")
    width = qkv_weight.shape[2]
    cond = time_emb.shape[1]
    hidden = up_weight.shape[1]
    n_bits = n_dp.bit_length() - 1
    assert lax.axis_size("tensor") == 4 and time_emb.shape[0] == 2 and 2 * rows == LEN
    assert n_dp == 1 << n_bits and n_bits >= HALVED and 4 * width == hidden == 3 * PIECE == d
    wt = qkv_weight.transpose(1, 2, 0).reshape(3 * width, d)
    table = jnp.asarray(rotary_block())
    a = pl.BlockSpec(memory_space=pl.ANY)
    m = pl.BlockSpec(memory_space=pltpu.VMEM)
    smem = pl.BlockSpec(memory_space=pltpu.SMEM)
    total = 4 * width + 2 * hidden
    noise = noise_mask.reshape(4, rows // 4)
    small_in = (mask_embed, gain_attn, gain_mlp, down_bias, up_bias, ada_bias, time_emb, noise)
    ins = [("tok_h", tokens, a), ("cot_h", cotangent, a), ("prefix", prefix_len, smem)]
    ins += [(name, value, a) for name, value in zip(SMALL_INPUTS, small_in)]
    ins += [("ada_h", ada_weight, a), ("table_h", table, a), ("wt_h", wt, a), ("wo_h", out_weight, a), ("wu_h", up_weight, a), ("wd_h", down_weight, a)]
    outs = [
        ("out_o", (rows, d), BF, a), ("gtok_o", (rows, d), F, a), ("grads_o", (total, d), BF, a), ("mods_o", (2 * n_dp, 8, d), F, a), ("small_o", (8, d), F, m),
        ("wmu", (4, d, hidden), BF, a), ("wmd", (4, hidden, d), BF, a),
    ]
    extra = max(n_bits - HALVED, 1)
    if n_bits > HALVED:
        outs.append(("ex", (extra, 9, 32, d), F, a))
    vmem = [
        ("w", (4, 4 * width, d), BF), ("wsu", (2, d, PIECE), BF), ("wsd", (2, PIECE, d), BF), ("rb", (2, 2 * hidden, d), BF), ("rx", (total, d), BF), ("sx", (total, d), BF),
        ("g0", (total, d), F), ("sb", (6 * PIECE, d), BF), ("ry", (9, 128, d), BF), ("rz1", (9, 64, d), BF), ("rz2", (9, 32, d), BF), ("exv", (32, d), F),
        ("tok", (rows, d), BF), ("cs", (2 * rows, 2 * HD), F), ("h1o", (rows, d), BF), ("h1p", (rows, d), BF),
        ("q", (4, rows, width), BF), ("k", (4, 2 * rows, width), BF), ("v", (4, 2 * rows, width), BF), ("att", (4, rows, width), BF), ("st", (4, 8, rows), F),
        ("km", (width // HD, 2 * rows, width), BF), ("branch", (rows, d), F), ("mixed", (rows, d), F), ("h2", (rows, d), BF), ("gm", (rows, d), BF),
        ("bm", (rows, d), F), ("gh", (rows, d), F), ("dk", (2 * rows, width), F), ("dv", (2 * rows, width), F), ("dq", (rows, width), F),
        ("parr", (2, rows, 2 * width), F), ("dwo2", (width, d), F), ("vecs", (8, d), F), ("mod", (8, d), F), ("nz", (rows, 1), F),
        ("bus", (4, 8, hidden), F), ("gub", (4, 8, hidden), F), ("sums", (16, d), F), ("mods", (2 * n_dp, 8, d), F), ("cse", (16, d), F), ("cre", (16, d), F),
        ("xse", (8, d), F), ("xre", (8, d), F), ("bse", (n_bits, 8, d), F), ("bre", (n_bits, 8, d), F),
    ]
    vmem += [(name + "_v", value.shape, value.dtype) for name, value in zip(SMALL_INPUTS, small_in)]
    pairs = [
        ("far", 10), ("side", 10), ("cross", 20), ("near", 4), ("bias", 3), ("h1", 1), ("give", 24), ("gx", 9), ("gy", 9), ("gz", 9), ("gw", 9), ("aw", 9), ("az", 9), ("ay", 9),
        ("ge", 9 * extra), ("par", 4), ("hand", 2), ("sc", 1), ("sx", 2), ("sd", 2 * n_bits),
    ]
    dma = pltpu.SemaphoreType.DMA
    sems = [("loc", dma((60,))), ("wst", dma((2, 2))), ("credit", pltpu.SemaphoreType.REGULAR)]
    for name, n in pairs:
        sems += [(name + "_s", dma((n,))), (name + "_r", dma((n,)))]
    names = [i[0] for i in ins] + [o[0] for o in outs] + [x[0] for x in vmem] + [x[0] for x in sems]
    res = pl.pallas_call(
        functools.partial(block_kernel, n_dp, names),
        out_shape=tuple(sds(shape, dtype) for _, shape, dtype, _ in outs),
        in_specs=[i[2] for i in ins],
        out_specs=tuple(o[3] for o in outs),
        scratch_shapes=[pltpu.VMEM(shape, dtype) for _, shape, dtype in vmem] + [x[1] for x in sems],
        compiler_params=pltpu.CompilerParams(vmem_limit_bytes=63 * MIB + 3 * MIB // 4, collective_id=0, has_side_effects=True),
        cost_estimate=pl.CostEstimate(flops=4 * 10**10, bytes_accessed=10**8, transcendentals=0),
        name="block",
    )(*[i[1] for i in ins])
    out16, gtok, grads, mods, small = res[:5]
    vecs = [sds((d,), F)] * 5
    finals = [sds((rows, d), BF), sds((rows, d), F), sds((3 * width, d), F), sds((width, d), F), sds((d, hidden), F), sds((hidden, d), F), sds((cond, 6 * d), F)]
    done = pl.pallas_call(
        functools.partial(finish_kernel, n_dp),
        out_shape=tuple(finals + [sds((2, cond), F), sds((6 * d,), F)] + vecs),
        in_specs=[a, a, a, a, m, a, m],
        out_specs=tuple([a] * len(finals) + [m] * 7),
        scratch_shapes=[
            pltpu.VMEM((total, d), BF), pltpu.VMEM((total, d), F), pltpu.VMEM((rows, d), BF), pltpu.VMEM((rows, d), F), pltpu.VMEM(mods.shape, F),
            pltpu.VMEM(ada_weight.shape, BF), pltpu.VMEM((6, cond, d), F), dma((40,)),
        ],
        compiler_params=pltpu.CompilerParams(vmem_limit_bytes=63 * MIB),
        cost_estimate=pl.CostEstimate(flops=10**8, bytes_accessed=2 * 10**7, transcendentals=0),
        name="finish",
    )(grads, out16, gtok, mods, small, ada_weight, time_emb)
    output, grad_tokens, gqkv, gout, gup, gdown, grad_ada, grad_time, grad_adab, g_mask, g_attn, g_mlp, g_upb, g_db = done
    return (output, grad_tokens, grad_time, g_mask, g_attn, g_mlp, grad_ada, grad_adab, gqkv.reshape(3, width, d).transpose(2, 0, 1), gout, gup, g_upb, gdown, g_db)


def solution(mesh):
    group = ("dp", "tensor")
    in_specs = (P(group, None), P("dp", None), P("dp"), P(group), P(), P(), P(), P(), P(), P(None, None, "tensor"), P("tensor", None), P(None, "tensor"), P("tensor"), P("tensor", None), P(), P(group, None))
    out_specs = (P(group, None), P(group, None), P("dp", None), P(), P(), P(), P(), P(), P(None, None, "tensor"), P("tensor", None), P(None, "tensor"), P("tensor"), P("tensor", None), P())
    return jax.shard_map(per_device, mesh=mesh, in_specs=in_specs, out_specs=out_specs, check_vma=False)
```

time: 905 us -> 195 us (0.22)
  waiting for transfers between devices: 572 us -> 0 us
  Pallas kernels: 0 us -> 194 us
  matrix products: 117 us -> 0 us
  blocking collectives: 74.1 us -> 0 us
  local copies, waits for them, and re-layouts: 60.8 us -> 0 us
  other arithmetic: 56.7 us -> 0 us
  between operations: 15.5 us -> 0.84 us
    psum x2 -> x0, waiting for transfers between devices: 306 us -> none  [the longest x1 165 us: per_device(): lax.psum((grad_qkv, grad_out_weight, grad_up, grad_up_bias, grad_down), '...]
    pallas_call x0 -> x2, Pallas kernels: none -> 194 us  [the longest x1 186 us: per_device(): pl.pallas_call(functools.partial(block_kernel, n_dp, names), out_shape=tu...]
    reduce_scatter x4 -> x0, waiting for transfers between devices: 162 us -> none  [the longest x1 57.9 us: per_device(): lax.psum_scatter(partial_attn, 'tensor', scatter_dimension=0, tiled=True)]
    dot_general x29 -> x0, matrix products: 108 us -> none  [the longest x3 17 us: contract_cols(): lax.dot_general(left, right, (((1,), (1,)), ((), ())), preferred_element_...]
    all_gather x4 -> x0, waiting for transfers between devices: 103 us -> none  [the longest x1 28.4 us: per_device(): lax.all_gather(grad_branch_attn, 'tensor', axis=0, tiled=True)]
    psum x3 -> x0, blocking collectives: 74.1 us -> none  [the longest x1 45.2 us: per_device(): lax.psum((grad_ada_weight, grad_ada_bias, grad_gain_one, grad_gain_two, g...]
    unnamed x152 -> x0, local copies, waits for them, and re-layouts: 34.3 us -> none
    reduce_sum x11 -> x0, other arithmetic: 26.5 us -> none  [the longest x1 4.65 us: per_device(): jnp.sum(grad_hidden_two * (1.0 + scale_mlp) * norm_two, axis=0)]
  transfers between devices with their start and end apart: 10 -> 0, of which waited for: 10 -> 0; matrix products, arithmetic and copies ran while one was open for 7% -> 0% of each run, Pallas kernels for 0% -> 0%
where the time goes in v2:
time: 195 us
  Pallas kernels  194 us (99%)
    pallas_call x1, Pallas kernels, per_device(): pl.pallas_call(functools.partial(block_kernel, n_dp, names), out_shape=tu...  186 us
    pallas_call x1, Pallas kernels, per_device(): pl.pallas_call(functools.partial(finish_kernel, n_dp), out_shape=tuple(fi...  7.78 us

profile of v2, /device:TPU:0, one launch (start us, length us, event | category | flops | bytes accessed | tf_op | source)
XLA Modules:
  0.0 195.1 jit_solution(7451208444346059183)
XLA Ops:
  0.7 186.4 %block.1 = (bf16[512,768]{1,0:T(8,128)(2,1)}, f32[512,768]{1,0:T(8,128)}, bf16[2304,768]{1,0:T(8,128)(2,1)}, f32[16,8,768]{2,1,0:T(8,128)}, f32[8,768]{1,0:T(8,1...) custom-call(bf16[512,768]{1,0:T(8,128)(2,1)} %args_0_.4, bf16[512,768]{1,0:T(8,128)(2,1)} %args_1_.4, ...), custom_call_target="tpu_custom_call" | custom-call | flops 40000000000 | bytes 100000000 | tf_op jit(solution)/shard_map/block/pallas_call | solution.py:956
  187.1 7.8 %finish.1 = (bf16[512,768]{1,0:T(8,128)(2,1)}, f32[512,768]{1,0:T(8,128)}, f32[576,768]{1,0:T(8,128)}, f32[192,768]{1,0:T(8,128)}, f32[768,768]{1,0:T(8,128)}, /...) custom-call(bf16[2304,768]{1,0:T(8,128)(2,1)} %get-tuple-element.33., ...), custom_call_target="tpu_custom_call" | custom-call | flops 100000000 | bytes 20000000 | tf_op jit(solution)/shard_map/finish/pallas_call | solution.py:969

commit v3 on v2

--- a/solution.py
+++ b/solution.py
@@ -90,8 +90,8 @@
     return out
 
 
-MLP_ORDER = [(1, 0), (1, 1), (1, 2), (3, 0), (2, 0), (0, 0), (0, 1), (3, 1), (2, 1), (0, 2), (3, 2), (2, 2)]
-CROSS = [3, 6, 4, 7, 5, 8, 0, 1, 2]
+MLP_ORDER = [(1, 0), (1, 1), (3, 0), (2, 0), (1, 2), (0, 0), (3, 1), (2, 1), (0, 1), (0, 2), (3, 2), (2, 2)]
+CROSS = [(768, 256), (1536, 256), (1024, 256), (1792, 256), (1280, 256), (2048, 256), (0, 128), (128, 128), (256, 128), (384, 128), (512, 128), (640, 128)]
 SMALL_INPUTS = ("mask", "gain1", "gain2", "dbias", "upb", "adab", "time", "noise")
 
 
@@ -100,7 +100,7 @@
     g = lambda *keys: [ref[key] for key in keys]
     tok_h, cot_h, prefix, ada_h, table_h, wt_h, wo_h, wu_h, wd_h = g("tok_h", "cot_h", "prefix", "ada_h", "table_h", "wt_h", "wo_h", "wu_h", "wd_h")
     out_o, gtok_o, grads_o, mods_o, small_o, wmu, wmd = g("out_o", "gtok_o", "grads_o", "mods_o", "small_o", "wmu", "wmd")
-    w, wsu, wsd, rb, rx, sx, g0, sb, ry, rz1, rz2, exv = g("w", "wsu", "wsd", "rb", "rx", "sx", "g0", "sb", "ry", "rz1", "rz2", "exv")
+    w, wsu, wsd, rb, rx, sx, g0, sb, ry, rz, exv = g("w", "wsu", "wsd", "rb", "rx", "sx", "g0", "sb", "ry", "rz", "exv")
     tok, cs, h1o, h1p, q, k, v, att, st, km = g("tok", "cs", "h1o", "h1p", "q", "k", "v", "att", "st", "km")
     branch, mixed, h2, gm, bm, gh, dk, dv, dq, parr, dwo2 = g(
         "branch", "mixed", "h2", "gm", "bm", "gh", "dk", "dv", "dq", "parr", "dwo2"
@@ -123,10 +123,11 @@
     peer = [(dp + b - 2 * b * v_, t) for b, v_ in zip(bits, bit)]
     yb = bit[0]
 
+    corner = (dp + 2 - 4 * bit[1] + 4 - 8 * bit[2], t)
     barrier = pltpu.get_barrier_semaphore()
-    for other in [core, chip] + peer:
+    for other in [core, chip, corner] + peer:
         pl.semaphore_signal(barrier, inc=1, device_id=other, device_id_type=MESH)
-    pl.semaphore_wait(barrier, 2 + len(peer))
+    pl.semaphore_wait(barrier, 3 + len(peer))
 
     def remote(src, dst, name, index, to):
         return pltpu.make_async_remote_copy(
@@ -356,116 +357,119 @@
     load_cot = local(cot_h, tok, 7)
     load_cot.start()
 
-    def piece(buf, p, start=0, size=PIECE):
-        return buf.at[at(p * PIECE + start, size)]
-
     def cross_send(n):
-        p = CROSS[n]
-        return remote(piece(sx, p), piece(rx, p), "gx", p, chip)
-
-    off1 = yb * 128
-    off2 = off1 + bit[1] * 64
-    off3 = off2 + bit[2] * 32
-    anti1 = (1 - yb) * 128
-    anti2 = off1 + (1 - bit[1]) * 64
-    anti3 = off2 + (1 - bit[2]) * 32
-
-    def sl(p, start, size):
-        return at(p * PIECE + start, size, 32)
-
-    def send_y(p):
-        return remote(rx.at[pl.ds(p * PIECE, 128)], ry.at[p], "gy", p, peer[0])
-
-    def send_z1(p):
-        return remote(rx.at[pl.ds(p * PIECE + 128, 64)], rz1.at[p], "gz", p, peer[1])
-
-    def send_z2(p):
-        return remote(rx.at[pl.ds(p * PIECE + 192, 32)], rz2.at[p], "gw", p, peer[2])
-
-    def back_z2(p):
-        return remote(sx.at[sl(p, off3, 32)], sx.at[sl(p, off3, 32)], "aw", p, peer[2])
-
-    def back_z1(p):
-        return remote(sx.at[sl(p, off2, 64)], sx.at[sl(p, off2, 64)], "az", p, peer[1])
-
-    def back_y(p):
-        return remote(sx.at[sl(p, off1, 128)], sx.at[sl(p, off1, 128)], "ay", p, peer[0])
-
-    def more(e, p):
-        return remote(g0.at[sl(p, off3, 32)], ref["ex"].at[e, p], "ge", e * 9 + p, peer[HALVED + e])
+        base, size = CROSS[n]
+        return remote(sx.at[pl.ds(base, size)], rx.at[pl.ds(base, size)], "gx", n, chip)
+
+    def line_peer(m):
+        return (dp + (2 - 4 * bit[1] if m & 2 else 0) + (4 - 8 * bit[2] if m & 1 else 0), t)
+
+    def half_at(n, other=False):
+        base, size = CROSS[n]
+        return at(base + ((1 - yb) if other else yb) * (size // 2), size // 2, 16)
+
+    def line_at(n, m=0):
+        base, size = CROSS[n]
+        rank = 2 * (1 - bit[1] if m & 2 else bit[1]) + (1 - bit[2] if m & 1 else bit[2])
+        return at(base + yb * (size // 2) + rank * (size // 8), size // 8, 16)
+
+    def out_half(n):
+        base, size = CROSS[n]
+        return pl.ds(base, size // 2)
+
+    def out_line(n, m):
+        base, size = CROSS[n]
+        return pl.ds(base + size // 2 + (m - 1) * (size // 8), size // 8)
+
+    def in_half(n):
+        base, size = CROSS[n]
+        return pl.ds(base // 2, size // 2)
+
+    def in_line(n, m):
+        base, size = CROSS[n]
+        return pl.ds(base * 3 // 8 + (m - 1) * (size // 8), size // 8)
+
+    def send_y(n):
+        return remote(rx.at[out_half(n)], ry.at[in_half(n)], "gy", n, peer[0])
+
+    def send_line(n, m):
+        return remote(rx.at[out_line(n, m)], rz.at[in_line(n, m)], "gz", 3 * n + m - 1, line_peer(m))
+
+    def back_far(n):
+        return remote(sx.at[line_at(n)], sx.at[line_at(n)], "aw", n, peer[2])
+
+    def back_near(n):
+        base, size = CROSS[n]
+        two = at(base + yb * (size // 2) + bit[1] * (size // 4), size // 4, 16)
+        return remote(sx.at[two], sx.at[two], "az", n, peer[1])
+
+    def back_y(n):
+        return remote(sx.at[half_at(n)], sx.at[half_at(n)], "ay", n, peer[0])
+
+    def more(e, n):
+        return remote(g0.at[line_at(n)], ref["ex"].at[e, n, pl.ds(0, CROSS[n][1] // 8)], "ge", e * len(CROSS) + n, peer[HALVED + e])
 
     def stage_x(n):
-        p = CROSS[n]
+        base, size = CROSS[n]
         cross_send(n).wait()
-        g0[piece_ds(p), :] = g0[piece_ds(p), :] + rx[piece_ds(p), :].astype(F)
-        rx[pl.ds(p * PIECE, 128), :] = g0[sl(p, anti1, 128), :].astype(BF)
-        send_y(p).start()
-
-    def piece_ds(p):
-        return pl.ds(p * PIECE, PIECE)
+        g0[pl.ds(base, size), :] = g0[pl.ds(base, size), :] + rx[pl.ds(base, size), :].astype(F)
+        rx[out_half(n), :] = g0[half_at(n, True), :].astype(BF)
+        send_y(n).start()
 
     def stage_y(n):
-        p = CROSS[n]
-        send_y(p).wait_recv()
-        g0[sl(p, off1, 128), :] = g0[sl(p, off1, 128), :] + ry[p].astype(F)
-        rx[pl.ds(p * PIECE + 128, 64), :] = g0[sl(p, anti2, 64), :].astype(BF)
-        send_z1(p).start()
-
-    def stage_z1(n):
-        p = CROSS[n]
-        send_z1(p).wait_recv()
-        g0[sl(p, off2, 64), :] = g0[sl(p, off2, 64), :] + rz1[p].astype(F)
-        rx[pl.ds(p * PIECE + 192, 32), :] = g0[sl(p, anti3, 32), :].astype(BF)
-        send_z2(p).start()
-
-    def stage_z2(n):
-        p = CROSS[n]
-        send_z2(p).wait_recv()
-        total = g0[sl(p, off3, 32), :] + rz2[p].astype(F)
+        send_y(n).wait_recv()
+        g0[half_at(n), :] = g0[half_at(n), :] + ry[in_half(n), :].astype(F)
+        for m in (1, 2, 3):
+            rx[out_line(n, m), :] = g0[line_at(n, m), :].astype(BF)
+            send_line(n, m).start()
+
+    def stage_z(n):
+        for m in (1, 2, 3):
+            send_line(n, m).wait_recv()
+        got = [rz[in_line(n, m), :].astype(F) for m in (1, 2, 3)]
+        total = g0[line_at(n), :] + ((got[0] + got[1]) + got[2])
         for e in range(len(bits) - HALVED):
-            g0[sl(p, off3, 32), :] = total
-            more(e, p).start()
-            more(e, p).wait()
-            fill = local(ref["ex"].at[e, p], exv, 36)
+            g0[line_at(n), :] = total
+            more(e, n).start()
+            more(e, n).wait()
+            room = pl.ds(0, CROSS[n][1] // 8)
+            fill = local(ref["ex"].at[e, n, room], exv.at[room], 36)
             fill.start()
             fill.wait()
-            total = total + exv[...]
-        sx[sl(p, off3, 32), :] = total.astype(BF)
-        back_z2(p).start()
-
-    def stage_a1(n):
-        p = CROSS[n]
-        back_z2(p).wait_recv()
-        back_z1(p).start()
-
-    def stage_a2(n):
-        p = CROSS[n]
-        back_z1(p).wait_recv()
-        back_y(p).start()
-
-    def result(p):
-        return local(sx.at[piece_ds(p)], grads_o.at[piece_ds(p)], 14 + p)
-
-    def stage_a3(n):
-        p = CROSS[n]
-        back_y(p).wait_recv()
-        result(p).start()
+            total = total + exv[room, :]
+        sx[line_at(n), :] = total.astype(BF)
+        back_far(n).start()
+
+    def stage_a(n):
+        back_far(n).wait_recv()
+        back_near(n).start()
+
+    def stage_b(n):
+        back_near(n).wait_recv()
+        back_y(n).start()
+
+    def result(n):
+        base, size = CROSS[n]
+        return local(sx.at[pl.ds(base, size)], grads_o.at[pl.ds(base, size)], 14 + n)
+
+    def stage_c(n):
+        back_y(n).wait_recv()
+        result(n).start()
 
     def stage_end(n):
-        p = CROSS[n]
-        send_y(p).wait_send()
-        send_z1(p).wait_send()
-        send_z2(p).wait_send()
-        back_z2(p).wait_send()
-        back_z1(p).wait_send()
-        back_y(p).wait_send()
-        result(p).wait()
-
-    stages = dict(X=stage_x, Y=stage_y, Z=stage_z1, W=stage_z2, A=stage_a1, B=stage_a2, C=stage_a3, E=stage_end)
+        send_y(n).wait_send()
+        for m in (1, 2, 3):
+            send_line(n, m).wait_send()
+        back_far(n).wait_send()
+        back_near(n).wait_send()
+        back_y(n).wait_send()
+        result(n).wait()
+
+    stages = dict(X=stage_x, Y=stage_y, Z=stage_z, A=stage_a, B=stage_b, C=stage_c)
 
     def run(text):
         for i in range(0, len(text), 2):
-            stages[text[i]](int(text[i + 1]))
+            stages[text[i]](int(text[i + 1], 16))
 
     steps = len(MLP_ORDER)
 
@@ -495,11 +499,11 @@
         c.start()
 
     mlp_plan = {
-        1: [go_on(5), arrive(7)],
-        2: [wait_cross(4), wait_cross(5), go_on(6)],
-        4: [arrive(8), go_on(7)],
-        6: [wait_cross(6), wait_cross(7), arrive(9)],
-        8: [go_on(8)],
+        0: [go_on(5)],
+        1: [wait_cross(4), wait_cross(5), arrive(7), go_on(6)],
+        3: [arrive(8), go_on(7)],
+        5: [wait_cross(6), wait_cross(7), arrive(9)],
+        7: [go_on(8)],
         9: [go_on(9), wait_cross(8), wait_cross(9)],
     }
 
@@ -558,7 +562,7 @@
                         total = ds_[kind] + rb[r_ // 2, inbox[kind], :].astype(F)
                         if r_ == 2:
                             sx[rows_[kind], :] = total.astype(BF)
-                            cross_send(CROSS.index(3 + 3 * kind + c_)).start()
+                            cross_send(CROSS.index(((3 + 3 * kind + c_) * PIECE, PIECE))).start()
                         else:
                             g0[rows_[kind], :] = total
 
@@ -605,7 +609,6 @@
     store_out.start()
     load_tok = local(tok_h, tok, 6)
     load_tok.start()
-    run("")
     for r in range(4):
         wo = w[r, 3 * width : 4 * width, :]
         dw = tn(att[r], gba[...])
@@ -696,7 +699,7 @@
             hand(r).start()
         elif r == 2:
             sx[place_, :] = (dwo2[...] + rb[1, place_, :].astype(F)).astype(BF)
-            for n in (6, 7, 8):
+            for n in range(6, len(CROSS)):
                 cross_send(n).start()
         else:
             g0[place_, :] = g0[place_, :] + rb[0, place_, :].astype(F)
@@ -705,9 +708,9 @@
         pl.semaphore_signal(ref["credit"], inc=1, device_id=core, device_id_type=MESH)
 
     back_plan = [
-        {0: "X1Y0", 2: "X2", 4: "W1X3", 5: "Z2A1Y3X4", 6: "W2"},
-        {1: "Z0", 2: "W0", 3: "A0", 4: "B0", 5: "C0", 6: "B1", 7: "A2"},
-        {1: "Y1", 2: "Z1", 3: "Y2", 6: "Y4X5Z3", 7: "C1Z4"},
+        {0: "X1", 2: "Y1X2", 4: "Z1Y2", 5: "A1Y3X4B0Z2", 7: "Y4Z3X5"},
+        {4: "X3A0", 6: "B1", 7: "A2"},
+        {0: "Y0", 2: "Z0"},
     ]
 
     def back_events(it, h):
@@ -731,16 +734,16 @@
         return carry
 
     lax.fori_loop(0, 4 * per_r, back_body, 0)
-    run("")
+    run("C0")
     weight_grads(1)
-    run("W3Y5B2")
+    run("Z4C1")
     weight_grads(0)
 
     hand(1).wait_send()
     hand(3).wait_send()
     store_out.wait()
     load_tok.wait()
-    run("X6W4")
+    run("X6X7B2A3Y5X8")
 
     def tail_body(i, carry):
         rs = at(i * tile, tile, tile)
@@ -767,58 +770,67 @@
     lax.fori_loop(0, per_r, tail_body, 0)
     store_tok = local(mixed, gtok_o, 27)
     store_tok.start()
-    run("A3C2Z5")
+    run("A4")
 
     none = jnp.zeros((2, d), F)
     cse[0:8, :] = jnp.concatenate([sums[8:14, :], none], axis=0)
     cse[8:16, :] = jnp.concatenate([gub[1, 0:1, :], gub[3, 0:1, :], sums[1:5, :], none], axis=0)
     core_sum = remote(cse, cre, "sc", 0, core)
     core_sum.start()
-    run("")
-    core_sum.wait_recv()
-    own_mods = cse[0:6, :] + cre[0:6, :]
-    tv_row = jnp.concatenate([tv, jnp.zeros((1, d - cond), F)], axis=1)
     me = 2 * dp + xb
-    mods[me] = jnp.concatenate([own_mods, tv_row, jnp.zeros((1, d), F)], axis=0)
-    xse[...] = jnp.concatenate([gub[2, 0:1, :] + cre[9:10, :], cse[10:14, :] + cre[10:14, :], jnp.zeros((3, d), F)], axis=0)
     chip_sum = remote(xse, xre, "sx", 0, chip)
     chip_mods = remote(mods.at[me], mods.at[me], "sx", 1, chip)
-    chip_sum.start()
-    chip_mods.start()
-    run("X7A4Y6B3")
-    chip_sum.wait_recv()
-    cur = jnp.concatenate([gub[0, 0:1, :] + cre[8:9, :] + xre[0:1, :], xse[1:8, :] + xre[1:8, :]], axis=0)
-    chip_mods.wait()
-    pending = [core_sum, chip_sum]
-    drain = ["W5", "B4", "Y7X8Z6"]
-    for i, b in enumerate(bits):
-        bse[i] = cur
-        base = (dp // b) * b * 2
-        one = remote(bse.at[i], bre.at[i], "sd", 2 * i, peer[i])
-        two = remote(mods.at[pl.ds(base, 2 * b)], mods.at[pl.ds(base, 2 * b)], "sd", 2 * i + 1, peer[i])
-        one.start()
-        two.start()
-        if drain:
-            run(drain.pop(0))
-        one.wait_recv()
-        two.wait()
-        pending.append(one)
-        cur = cur + bre[i]
-    small_o[...] = cur
-    for text in drain:
-        run(text)
+
+    def peer_sums(i):
+        block = pl.ds((dp // bits[i]) * bits[i] * 2, 2 * bits[i])
+        return remote(bse.at[i], bre.at[i], "sd", 2 * i, peer[i]), remote(mods.at[block], mods.at[block], "sd", 2 * i + 1, peer[i])
+
+    def sums_on(i):
+        if i == 0:
+            core_sum.wait_recv()
+            tv_row = jnp.concatenate([tv, jnp.zeros((1, d - cond), F)], axis=1)
+            mods[me] = jnp.concatenate([cse[0:6, :] + cre[0:6, :], tv_row, jnp.zeros((1, d), F)], axis=0)
+            xse[...] = jnp.concatenate([gub[2, 0:1, :] + cre[9:10, :], cse[10:14, :] + cre[10:14, :], jnp.zeros((3, d), F)], axis=0)
+            chip_sum.start()
+            chip_mods.start()
+            return
+        if i == 1:
+            chip_sum.wait_recv()
+            cur = jnp.concatenate([gub[0, 0:1, :] + cre[8:9, :] + xre[0:1, :], xse[1:8, :] + xre[1:8, :]], axis=0)
+            chip_mods.wait()
+        else:
+            one, two = peer_sums(i - 2)
+            one.wait_recv()
+            two.wait()
+            cur = bse[i - 2] + bre[i - 2]
+        if i - 1 < len(bits):
+            bse[i - 1] = cur
+            for c in peer_sums(i - 1):
+                c.start()
+        else:
+            small_o[...] = cur
+
+    run("Y6X9B3Y7")
+    sums_on(0)
+    run("Z5XaB4C2Z6Y8")
+    sums_on(1)
+    run("XbZ7A5Y9A6Z8C3A7")
+    for i in range(2, len(bits) - 1):
+        sums_on(i)
+    run("B5YaZ9B6A8B7C4Za")
+    sums_on(len(bits) - 1)
+    run("YbA9B8AaC5ZbB9C6")
+    sums_on(len(bits))
+    run("BaC7AbC8C9Bb")
+    sums_on(len(bits) + 1)
     store_mods = local(mods, mods_o, 28)
     store_mods.start()
-    run("A5C3Z7W6")
-    run("C4B5W7Y8")
-    run("A6A7C5Z8")
-    run("B6B7W8C6")
-    run("A8C7B8C8")
-    for n in range(9):
+    run("CaCb")
+    for n in range(len(CROSS)):
         stage_end(n)
     for c in [store_mods, store_tok]:
         c.wait()
-    for c in pending:
+    for c in [core_sum, chip_sum] + [peer_sums(i)[0] for i in range(len(bits))]:
         c.wait_send()
     for c in near + [bias_near, bias_far, bias_cross]:
         c.wait_send()
@@ -929,12 +941,13 @@
         ("out_o", (rows, d), BF, a), ("gtok_o", (rows, d), F, a), ("grads_o", (total, d), BF, a), ("mods_o", (2 * n_dp, 8, d), F, a), ("small_o", (8, d), F, m),
         ("wmu", (4, d, hidden), BF, a), ("wmd", (4, hidden, d), BF, a),
     ]
+    n_pieces = len(CROSS)
     extra = max(n_bits - HALVED, 1)
     if n_bits > HALVED:
-        outs.append(("ex", (extra, 9, 32, d), F, a))
+        outs.append(("ex", (extra, n_pieces, 32, d), F, a))
     vmem = [
         ("w", (4, 4 * width, d), BF), ("wsu", (2, d, PIECE), BF), ("wsd", (2, PIECE, d), BF), ("rb", (2, 2 * hidden, d), BF), ("rx", (total, d), BF), ("sx", (total, d), BF),
-        ("g0", (total, d), F), ("sb", (6 * PIECE, d), BF), ("ry", (9, 128, d), BF), ("rz1", (9, 64, d), BF), ("rz2", (9, 32, d), BF), ("exv", (32, d), F),
+        ("g0", (total, d), F), ("sb", (6 * PIECE, d), BF), ("ry", (total // 2, d), BF), ("rz", (total * 3 // 8, d), BF), ("exv", (32, d), F),
         ("tok", (rows, d), BF), ("cs", (2 * rows, 2 * HD), F), ("h1o", (rows, d), BF), ("h1p", (rows, d), BF),
         ("q", (4, rows, width), BF), ("k", (4, 2 * rows, width), BF), ("v", (4, 2 * rows, width), BF), ("att", (4, rows, width), BF), ("st", (4, 8, rows), F),
         ("km", (width // HD, 2 * rows, width), BF), ("branch", (rows, d), F), ("mixed", (rows, d), F), ("h2", (rows, d), BF), ("gm", (rows, d), BF),
@@ -945,8 +958,8 @@
     ]
     vmem += [(name + "_v", value.shape, value.dtype) for name, value in zip(SMALL_INPUTS, small_in)]
     pairs = [
-        ("far", 10), ("side", 10), ("cross", 20), ("near", 4), ("bias", 3), ("h1", 1), ("give", 24), ("gx", 9), ("gy", 9), ("gz", 9), ("gw", 9), ("aw", 9), ("az", 9), ("ay", 9),
-        ("ge", 9 * extra), ("par", 4), ("hand", 2), ("sc", 1), ("sx", 2), ("sd", 2 * n_bits),
+        ("far", 10), ("side", 10), ("cross", 20), ("near", 4), ("bias", 3), ("h1", 1), ("give", 24), ("gx", n_pieces), ("gy", n_pieces), ("gz", 3 * n_pieces), ("aw", n_pieces), ("az", n_pieces), ("ay", n_pieces),
+        ("ge", n_pieces * extra), ("par", 4), ("hand", 2), ("sc", 1), ("sx", 2), ("sd", 2 * n_bits),
     ]
     dma = pltpu.SemaphoreType.DMA
     sems = [("loc", dma((60,))), ("wst", dma((2, 2))), ("credit", pltpu.SemaphoreType.REGULAR)]

time: 195 us -> 181 us (0.928)
  Pallas kernels: 194 us -> 180 us
    pallas_call x1, Pallas kernels: 186 us -> 173 us  [per_device(): pl.pallas_call(functools.partial(block_kernel, n_dp, names), out_shape=tu...]
where the time goes in v3:
time: 181 us
  Pallas kernels  180 us (99%)
    pallas_call x1, Pallas kernels, per_device(): pl.pallas_call(functools.partial(block_kernel, n_dp, names), out_shape=tu...  173 us
    pallas_call x1, Pallas kernels, per_device(): pl.pallas_call(functools.partial(finish_kernel, n_dp), out_shape=tuple(fi...  7.78 us

profile of v3, /device:TPU:0, one launch (start us, length us, event | category | flops | bytes accessed | tf_op | source)
XLA Modules:
  0.0 181.1 jit_solution(11911517465342212030)
XLA Ops:
  0.7 172.5 %block.1 = (bf16[512,768]{1,0:T(8,128)(2,1)}, f32[512,768]{1,0:T(8,128)}, bf16[2304,768]{1,0:T(8,128)(2,1)}, f32[16,8,768]{2,1,0:T(8,128)}, f32[8,768]{1,0:T(8,1...) custom-call(bf16[512,768]{1,0:T(8,128)(2,1)} %args_0_.4, bf16[512,768]{1,0:T(8,128)(2,1)} %args_1_.4, ...), custom_call_target="tpu_custom_call" | custom-call | flops 40000000000 | bytes 100000000 | tf_op jit(solution)/shard_map/block/pallas_call | solution.py:969
  173.2 7.8 %finish.1 = (bf16[512,768]{1,0:T(8,128)(2,1)}, f32[512,768]{1,0:T(8,128)}, f32[576,768]{1,0:T(8,128)}, f32[192,768]{1,0:T(8,128)}, f32[768,768]{1,0:T(8,128)}, /...) custom-call(bf16[2304,768]{1,0:T(8,128)(2,1)} %get-tuple-element.33., ...), custom_call_target="tpu_custom_call" | custom-call | flops 100000000 | bytes 20000000 | tf_op jit(solution)/shard_map/finish/pallas_call | solution.py:982

commit v4 on v3

--- a/solution.py
+++ b/solution.py
@@ -843,7 +843,7 @@
         par_copy(r).wait_send()
 
 
-def finish_kernel(n_dp, grads_h, out_h, tok_h, mods_h, small, ada_h, time, out_o, gtok_o, gqkv_o, gout_o, gup_o, gdown_o, gada_o, gtime_o, gadab_o, gmask_o, ga_o, gm_o, gub_o, gdb_o, grads, wide, outv, tokv, mods, ada, adag, sem):
+def finish_kernel(n_dp, grads_h, out_h, tok_h, mods_h, small_h, ada_h, time_h, out_o, gtok_o, gqkv_o, gout_o, gup_o, gdown_o, gada_o, gtime_o, gadab_o, gmask_o, ga_o, gm_o, gub_o, gdb_o, grads, wide, outv, tokv, mods, ada, adag, small, time, gtv, gbv, row0, row1, row2, row3, row4, sem):
     d = grads.shape[1]
     width = gout_o.shape[0]
     cond = ada.shape[0]
@@ -857,14 +857,21 @@
     load_mods, load_ada = copy(mods_h, mods, 0), copy(ada_h, ada, 1)
     load_tok, load_out = copy(tok_h, tokv, 2), copy(out_h, outv, 3)
     pieces = [copy(grads_h.at[span(p)], grads.at[span(p)], 4 + p) for p in range(9)]
-    for c in [load_mods] + pieces + [load_tok, load_out, load_ada]:
+    rowv = (row0, row1, row2, row3, row4)
+    load_small = [copy(small_h, small, 36), copy(time_h, time, 37)]
+    for c in load_small + [load_mods] + pieces + [load_tok, load_out, load_ada]:
         c.start()
     stores = []
 
     def store(src, dst):
-        stores.append(copy(src, dst, 13 + len(stores)))
+        stores.append(copy(src, dst, 13 + len(stores) if len(stores) < 23 else 15 + len(stores)))
         stores[-1].start()
 
+    for c in load_small:
+        c.wait()
+    for row, o in enumerate((gub_o, ga_o, gmask_o, gm_o, gdb_o)):
+        rowv[row][...] = small[row : row + 1, :].reshape(d)
+        store(rowv[row], o)
     head = 3 * width
     for p in range(9):
         pieces[p].wait()
@@ -891,7 +898,7 @@
     left = split3(tall / (1.0 + jnp.exp(-tall)))
     lhs = jnp.concatenate([left[0], left[0], left[1], left[0], left[2], left[1]], axis=0).astype(BF)
     for j in range(6):
-        gadab_o[pl.ds(j * d, d)] = total[j : j + 1, :].reshape(d)
+        gbv[pl.ds(j * d, d)] = total[j : j + 1, :].reshape(d)
         right = split3(jnp.concatenate([mods[s_, j : j + 1, :] for s_ in range(seqs)], axis=0))
         rhs = jnp.concatenate([right[0], right[1], right[0], right[2], right[0], right[1]], axis=0).astype(BF)
         adag[j] = tn(lhs, rhs)
@@ -903,9 +910,9 @@
         acc = acc + nt(jnp.concatenate(split3(pairs), axis=0).astype(BF), ada[:, pl.ds(j * d, d)])
     te = time[...].astype(F)
     sig = 1.0 / (1.0 + jnp.exp(-te))
-    gtime_o[...] = (acc[0:2] + acc[16:18] + acc[32:34]) * sig * (1.0 + te * (1.0 - sig))
-    for row, o in enumerate((gub_o, ga_o, gmask_o, gm_o, gdb_o)):
-        o[...] = small[row : row + 1, :].reshape(d)
+    gtv[...] = (acc[0:2] + acc[16:18] + acc[32:34]) * sig * (1.0 + te * (1.0 - sig))
+    store(gtv, gtime_o)
+    store(gbv, gadab_o)
     for c in stores:
         c.wait()
 
@@ -982,11 +989,12 @@
     done = pl.pallas_call(
         functools.partial(finish_kernel, n_dp),
         out_shape=tuple(finals + [sds((2, cond), F), sds((6 * d,), F)] + vecs),
-        in_specs=[a, a, a, a, m, a, m],
-        out_specs=tuple([a] * len(finals) + [m] * 7),
+        in_specs=[a] * 7,
+        out_specs=tuple([a] * (len(finals) + 7)),
         scratch_shapes=[
             pltpu.VMEM((total, d), BF), pltpu.VMEM((total, d), F), pltpu.VMEM((rows, d), BF), pltpu.VMEM((rows, d), F), pltpu.VMEM(mods.shape, F),
-            pltpu.VMEM(ada_weight.shape, BF), pltpu.VMEM((6, cond, d), F), dma((40,)),
+            pltpu.VMEM(ada_weight.shape, BF), pltpu.VMEM((6, cond, d), F), pltpu.VMEM((8, d), F), pltpu.VMEM((2, cond), BF), pltpu.VMEM((2, cond), F), pltpu.VMEM((6 * d,), F),
+            *[pltpu.VMEM((d,), F)] * 5, dma((60,)),
         ],
         compiler_params=pltpu.CompilerParams(vmem_limit_bytes=63 * MIB),
         cost_estimate=pl.CostEstimate(flops=10**8, bytes_accessed=2 * 10**7, transcendentals=0),

time: 181 us -> 181 us (level)
  no operation moved by 1% of the time
where the time goes in v4:
time: 181 us; the launch traced here: 180 us
  Pallas kernels  180 us (99%)
    pallas_call x1, Pallas kernels, per_device(): pl.pallas_call(functools.partial(block_kernel, n_dp, names), out_shape=tu...  173 us
    pallas_call x1, Pallas kernels, per_device(): pl.pallas_call(functools.partial(finish_kernel, n_dp), out_shape=tuple(fi...  7.01 us

profile of v4, /device:TPU:0, one launch (start us, length us, event | category | flops | bytes accessed | tf_op | source)
XLA Modules:
  0.0 180.4 jit_solution(16767706415189040255)
XLA Ops:
  0.7 172.5 %block.1 = (bf16[512,768]{1,0:T(8,128)(2,1)}, f32[512,768]{1,0:T(8,128)}, bf16[2304,768]{1,0:T(8,128)(2,1)}, f32[16,8,768]{2,1,0:T(8,128)}, f32[8,768]{1,0:T(8,1...) custom-call(bf16[512,768]{1,0:T(8,128)(2,1)} %args_0_.4, bf16[512,768]{1,0:T(8,128)(2,1)} %args_1_.4, ...), custom_call_target="tpu_custom_call" | custom-call | flops 40000000000 | bytes 100000000 | tf_op jit(solution)/shard_map/block/pallas_call | solution.py:976
  173.2 7.0 %finish.1 = (bf16[512,768]{1,0:T(8,128)(2,1)}, f32[512,768]{1,0:T(8,128)}, f32[576,768]{1,0:T(8,128)}, f32[192,768]{1,0:T(8,128)}, f32[768,768]{1,0:T(8,128)}, /...) custom-call(bf16[2304,768]{1,0:T(8,128)(2,1)} %get-tuple-element.33., ...), custom_call_target="tpu_custom_call" | custom-call | flops 100000000 | bytes 20000000 | tf_op jit(solution)/shard_map/finish/pallas_call | solution.py:989
